TPU v7x, 32 devices: a whole 2x2x4 slice. The times are simulated.
32 devices in a mesh: dp: 4 (over y, core), row: 2 (over x), col: 4 (over z).
Axes of the slice: x: 2, y: 2, z: 4, core: 2. Of those that a mesh axis runs over, the one named last changes fastest.
Arguments:
- source_rows: bfloat16 [1536, 12288], P(('dp', 'col'), 'row'), may hold values from -6 to 6
- segments: int32 [16, 96], P(('dp', 'col')), may hold values from 0 to 95, as said below
- send_slots: int32 [16, 4, 23], P(('dp', 'col')), may hold values from 0 to 95
- send_counts: int32 [4, 4, 4], P('col'), may hold values from 1 to 23, as said below
- block_weight: bfloat16 [16, 768, 3072], P('row', None, 'col'), may hold values from -0.21875 to 0.21875
- lowrank_in: bfloat16 [16, 768, 512], P('row'), may hold values from -0.0546875 to 0.0546875
- lowrank_out: bfloat16 [512, 16, 3072], P(None, 'row', 'col'), may hold values from -0.25 to 0.25
- cotangent: bfloat16 [768, 16, 3072], P('dp', 'row', 'col'), may hold values from -6 to 6
Outputs:
- activation: bfloat16 [768, 16, 3072], P('dp', 'row', 'col')
- input_grad: bfloat16 [768, 12288], P(('dp', 'col'), 'row')
- block_grad: float32 [768, 16, 3072], P('dp', 'row', 'col')
- lowrank_out_grad: float32 [512, 16, 3072], P('dp', 'row', 'col')
Inputs may be any that keep to these rules, and one draw needn't show every extreme that they name: For every col index c and destination e, the entries send_counts[c, :, e] sum to 48. `segments`: along one device's slots the ids never fall.
All inputs are finite; a program needn't handle non-finite values.
Results may differ from a plain program's by a relative error of at most 0.024.
Values may be sent and summed in bfloat16 or wider, within the bound.
A program may use at most 128 MiB of HBM per device.

v0:
```python
import jax
import jax.numpy as jnp
from jax import lax
from jax.sharding import PartitionSpec as P

TOK_DEV = 48


def gelu_pair(pre_act):
    cubic = pre_act * pre_act * pre_act
    tanh_val = jnp.tanh(0.7978845608 * (pre_act + 0.044715 * cubic))
    activation = 0.5 * pre_act * (1.0 + tanh_val)
    derivative = 0.5 * (1.0 + tanh_val) + 0.5 * pre_act * (
        1.0 - tanh_val * tanh_val
    ) * 0.7978845608 * (1.0 + 0.134145 * pre_act * pre_act)
    return (activation, derivative)


def doc_weights(segment_row, alive_count):
    slot_ids = jnp.arange(segment_row.shape[0], dtype=jnp.int32)
    is_alive = slot_ids < alive_count
    same_doc = (segment_row[:, None] == segment_row[None, :]) & is_alive[None, :]
    doc_length = jnp.sum(same_doc.astype(jnp.float32), axis=1)
    return (32.0 / (16.0 + doc_length)).astype(jnp.bfloat16)


def contract_last(left_side, right_side):
    return lax.dot_general(
        left_side, right_side, (((1,), (1,)), ((), ())), preferred_element_type=jnp.float32
    )


def row_total(partial_sum):
    return lax.psum(partial_sum.astype(jnp.bfloat16), "row").astype(jnp.float32)


def local(
    source_rows, segments, send_slots, send_counts, block_weight, lowrank_in, lowrank_out, cotangent
):
    n_data = lax.axis_size("dp")
    my_data = lax.axis_index("dp")
    count_table = send_counts[0]
    my_alive = jnp.sum(lax.dynamic_index_in_dim(count_table, my_data, 0, keepdims=False))
    weights = doc_weights(segments[0], my_alive)
    slot_table = send_slots[0]
    outgoing = jnp.take(source_rows, slot_table, axis=0)
    out_weights = jnp.take(weights, slot_table, axis=0)
    incoming, in_weights = (
        lax.all_to_all(outgoing, "dp", split_axis=0, concat_axis=0, tiled=True),
        lax.all_to_all(out_weights, "dp", split_axis=0, concat_axis=0, tiled=True),
    )
    capacity = slot_table.shape[1]
    arrivals = lax.dynamic_index_in_dim(count_table, my_data, 1, keepdims=False)
    starts = jnp.cumsum(arrivals) - arrivals
    positions = jnp.arange(TOK_DEV, dtype=jnp.int32)
    sender = jnp.sum((starts[None, :] <= positions[:, None]).astype(jnp.int32), axis=1) - 1
    offset = positions - jnp.take(starts, sender)
    flat_index = sender * capacity + offset
    my_rows = jnp.take(incoming.reshape(n_data * capacity, incoming.shape[2]), flat_index, axis=0)
    my_weights = jnp.take(in_weights.reshape(n_data * capacity), flat_index, axis=0)
    n_blocks, block_in, block_out = block_weight.shape
    rank_width = lowrank_in.shape[2]
    flat_in = lowrank_in.reshape(n_blocks * block_in, rank_width)
    flat_out = lowrank_out.reshape(rank_width, n_blocks * block_out)
    own_part = jnp.dot(my_rows, flat_in, preferred_element_type=jnp.float32)
    own_low = lax.psum(own_part.astype(jnp.bfloat16), "row")
    panel_rows, panel_low, panel_weights = (
        lax.all_gather(my_rows, "col", axis=0, tiled=True),
        lax.all_gather(own_low, "col", axis=0, tiled=True),
        lax.all_gather(my_weights, "col", axis=0, tiled=True),
    )
    group_rows = panel_rows.shape[0]
    panel_blocks = panel_rows.reshape(group_rows, n_blocks, block_in)
    pre_act = jnp.einsum(
        "tbi,bij->tbj", panel_blocks, block_weight, preferred_element_type=jnp.float32
    )
    low_product = jnp.dot(panel_low, flat_out, preferred_element_type=jnp.float32)
    pre_act = pre_act + low_product.reshape(group_rows, n_blocks, block_out)
    activation, derivative = gelu_pair(pre_act)
    act_out = activation.astype(jnp.bfloat16)
    grad_pre = (
        panel_weights.astype(jnp.float32)[:, None, None]
        * cotangent.astype(jnp.float32)
        * derivative
    ).astype(jnp.bfloat16)
    input_term = jnp.einsum(
        "tbj,bij->tbi", grad_pre, block_weight, preferred_element_type=jnp.float32
    )
    low_term = contract_last(
        grad_pre.reshape(TOK_DEV * lax.axis_size("col"), n_blocks * block_out), flat_out
    )
    own_terms = lax.psum_scatter(
        jnp.concatenate(
            [input_term.reshape(TOK_DEV * lax.axis_size("col"), n_blocks * block_in), low_term],
            axis=1,
        ).astype(jnp.bfloat16),
        "col",
        scatter_dimension=0,
        tiled=True,
    ).astype(jnp.float32)
    low_grad = row_total(own_terms[:, n_blocks * block_in :]).astype(jnp.bfloat16)
    input_grad = (own_terms[:, : n_blocks * block_in] + contract_last(low_grad, flat_in)).astype(
        jnp.bfloat16
    )
    block_term = jnp.einsum(
        "tbi,tbj->ibj", panel_blocks, grad_pre, preferred_element_type=jnp.float32
    )
    out_term = lax.dot_general(
        panel_low,
        grad_pre.reshape(group_rows, n_blocks * block_out),
        (((0,), (0,)), ((), ())),
        preferred_element_type=jnp.float32,
    )
    out_term = out_term.reshape(rank_width, n_blocks, block_out)
    block_grad, out_grad = (
        lax.psum_scatter(
            block_term.astype(jnp.bfloat16), "dp", scatter_dimension=0, tiled=True
        ).astype(jnp.float32),
        lax.psum_scatter(
            out_term.astype(jnp.bfloat16), "dp", scatter_dimension=0, tiled=True
        ).astype(jnp.float32),
    )
    return (act_out, input_grad, block_grad, out_grad)


def solution(mesh):
    in_specs = (
        P(("dp", "col"), "row"),
        P(("dp", "col"), None),
        P(("dp", "col"), None, None),
        P("col", None, None),
        P("row", None, "col"),
        P("row", None, None),
        P(None, "row", "col"),
        P("dp", "row", "col"),
    )
    out_specs = (
        P("dp", "row", "col"),
        P(("dp", "col"), "row"),
        P("dp", "row", "col"),
        P("dp", "row", "col"),
    )
    return jax.shard_map(local, mesh=mesh, in_specs=in_specs, out_specs=out_specs, check_vma=False)
```

profile of v0, /device:TPU:0, one launch (start us, length us, event | category | flops | bytes accessed | tf_op | source)
XLA Modules:
  0.0 327.1 jit_solution(13946688314438553399)
XLA Ops:
  7.2 0.8 compare_select_fusion.1
  8.1 1.3 dynamic-slice_reduce_fusion.1
  9.4 0.6 iota_compare_fusion.1
  10.0 0.9 convert_reduce_fusion
  11.0 1.2 gather_fusion.2
  12.3 0.7 and_select_fusion
  13.0 0.6 copy.55
  13.6 4.3 %all-to-all-start.1 = ((bf16[4,1,23]{2,1,0:T(2,128)(2,1)}), bf16[4,1,23]{2,1,0:T(2,128)(2,1)S(1)}, u32[]{:S(2)}, u32[]{:S(2)}) async-start(bf16[4,1,23]{2,1,0:T(2,128)(2,1)} %copy.55), calls=%async_computation.1 | async-start | bytes 4096 | tf_op jit(solution)/shard_map/all_to_all | solution.py:50
  17.8 0.9 dynamic-slice_reduce_fusion
  18.7 0.7 compare_and_fusion
  19.4 1.2 gather_fusion
  20.6 0.3 reshape.247
  21.0 1.2 broadcast_select_fusion
  22.4 3.5 %all-to-all-start = ((bf16[4,23,6144]{2,1,0:T(8,128)(2,1)}), bf16[4,23,6144]{2,1,0:T(8,128)(2,1)S(1)}, u32[]{:S(2)}, u32[]{:S(2)}) async-start(bf16[4,23,6144]{2,1,0:T(8,128)(2,1)} %broadcast_select_fusion), calls=%async_computation | async-start | bytes 2359296 | tf_op jit(solution)/shard_map/all_to_all | solution.py:49
  26.0 0.7 fusion.31
  26.7 2.6 fusion.29
  29.5 0.8 gather_fusion.3
  30.3 2.6 broadcast_select_fusion.2
  32.9 8.8 %all-to-all-done = bf16[4,23,6144]{2,1,0:T(8,128)(2,1)S(1)} async-done(((bf16[4,23,6144]{2,1,0:T(8,128)(2,1)}), bf16[4,23,6144]{2,1,0:T(8,128)(2,1)S(1)}, u32[]{:S(2)}, u32[]{:S(2)}) %all-to-all-start) | async-done | bytes 1130528 | tf_op jit(solution)/shard_map/all_to_all | solution.py:49
  41.7 0.4 reshape.228
  42.1 0.9 gather_fusion.1
  43.0 0.9 broadcast_select_fusion.1
  44.0 7.5 %copy.69 = bf16[64,8,8,768]{3,1,2,0:T(8,128)(2,1)} copy(bf16[64,8,8,768]{3,2,1,0:T(8,128)(2,1)} %bitcast.119) | data formatting | bytes 12582912
  51.4 8.8 %copy.54 = bf16[6144,512]{1,0:T(8,128)(2,1)} copy(bf16[6144,512]{0,1:T(8,128)(2,1)} %bitcast.115) | data formatting | bytes 12582912 | tf_op jit(solution)/shard_map/dot_general | solution.py:77
  60.2 0.6 dynamic-slice.2
  61.7 13.1 %all-reduce = bf16[192]{0:T(256)(128)(2,1)S(1)} all-reduce(bf16[192]{0:T(256)(128)(2,1)S(1)} %dynamic-update-slice), channel_id=1, replica_groups=mesh['dp'=4,'row'=2,'col'=4] {'col'}, use_global_device_ids=true, to_apply=%add | all-reduce | flops 192 | bytes 768
  74.8 4.0 %convolution_convert_fusion.1 = bf16[48,512]{1,0:T(8,128)(2,1)S(1)} fusion(bf16[48,6144]{1,0:T(8,128)(2,1)S(1)} %copy-done.2, bf16[6144,512]{1,0:T(8,128)(2,1)} %bitcast.113), kind=kOutput, calls=%fused_computation.35 | convolution fusion | flops 302014464 | bytes 6930432 | tf_op jit(solution)/shard_map/dot_general | solution.py:65
  78.8 8.6 %psum.14 = bf16[48,512]{1,0:T(8,128)(2,1)S(1)} all-reduce(bf16[48,512]{1,0:T(8,128)(2,1)S(1)} %convolution_convert_fusion.1), channel_id=1, replica_groups=mesh['dp'=4,'row'=2,'col'=4] {'row'}, use_global_device_ids=true, to_apply=%region_2.3 | all-reduce | flops 24576 | bytes 98304 | tf_op jit(solution)/shard_map/psum | solution.py:66
  87.4 14.8 %all_gather.10 = bf16[192,512]{1,0:T(8,128)(2,1)S(1)} all-gather(bf16[48,512]{1,0:T(8,128)(2,1)S(1)} %psum.14), channel_id=1, replica_groups=mesh['dp'=4,'row'=2,'col'=4] {'col'}, dimensions={0}, use_global_device_ids=true | all-gather | bytes 245760 | tf_op jit(solution)/shard_map/all_gather | solution.py:69
  102.2 6.5 %fusion.15 = f32[8,192,768]{2,1,0:T(8,128)S(1)} fusion(bf16[8,768,768]{2,1,0:T(8,128)(2,1)} %param.12, bf16[24,8,8,768]{3,2,1,0:T(8,128)(2,1)} %bitcast.116), kind=kOutput, calls=%fused_computation.27 | convolution fusion | flops 1811939328 | bytes 16515072 | tf_op jit(solution)/shard_map/tbi,bij->tbj/dot_general | solution.py:74
  108.8 7.9 %fusion.11 = (bf16[192,8,768]{2,0,1:T(8,128)(2,1)S(1)}, bf16[192,8,768]{2,0,1:T(8,128)(2,1)}) fusion(bf16[192,8,768]{2,1,0:T(8,128)(2,1)S(1)} %copy-done.4, f32[192]{0:T(256)S(1)} %convert_element_type.52, bf16[8,768,512]{2,1,0:T(8,128)(2,1)} %bitcast.120, bf16[192,512]{1,0:T(8,128)(2,1)S(1)} %all_gather.10, f32[8,192,768]{2,1,0:T(8,128)S(1)} %fusion.15), kind=kOutput, calls=%fused_computation.19 | convolution fusion | flops 1236271104 | bytes 18285312 | tf_op jit(solution)/shard_map/dot_general | solution.py:77
  116.7 3.2 convert_bitcast_fusion.1
  119.9 5.1 %fusion.22 = bf16[192,512]{1,0:T(8,128)(2,1)S(1)} fusion(bf16[192,8,768]{2,0,1:T(8,128)(2,1)S(1)} %get-tuple-element.26, bf16[512,8,768]{2,1,0:T(8,128)(2,1)} %param.14), kind=kOutput, calls=%fused_computation.34 | convolution fusion | flops 1208057856 | bytes 8847360 | tf_op jit(solution)/shard_map/dot_general | solution.py:28
  125.0 0.3 copy.67
  125.3 1.7 pad_maximum_fusion
  127.0 4.4 %convolution_convert_fusion = bf16[512,8,768]{2,0,1:T(8,128)(2,1)} fusion(bf16[192,512]{1,0:T(8,128)(2,1)S(1)} %all_gather.10, bf16[192,8,768]{2,0,1:T(8,128)(2,1)S(1)} %get-tuple-element.26), kind=kOutput, calls=%fused_computation.22 | convolution fusion | flops 1211105280 | bytes 8847360 | tf_op jit(solution)/shard_map/dot_general | solution.py:108
  131.7 6.8 %convert_bitcast_fusion = bf16[768,8,768]{0,2,1:T(8,128)(2,1)} fusion(bf16[192,8,768]{2,0,1:T(8,128)(2,1)S(1)} %get-tuple-element.26, bf16[24,8,8,768]{3,2,1,0:T(8,128)(2,1)} %bitcast.117), kind=kOutput, calls=%fused_computation.4 | convolution fusion | flops 1816657920 | bytes 14155776 | tf_op jit(solution)/shard_map/tbi,tbj->ibj/dot_general | solution.py:105
  138.5 13.2 %copy.60 = bf16[768,8,768]{2,1,0:T(8,128)(2,1)} copy(bf16[768,8,768]{0,2,1:T(8,128)(2,1)} %convert_bitcast_fusion) | data formatting | bytes 18874368 | tf_op jit(solution)/shard_map/convert_element_type | solution.py:117
  151.8 1.6 copy-done.3
  153.4 2.7 copy.63
  156.1 18.9 %reduce-scatter.4.cloned.1.call-done = bf16[48,6656]{1,0:T(8,128)(2,1)} async-done(((bf16[192,6656]{1,0:T(8,128)(2,1)}), bf16[48,6656]{1,0:T(8,128)(2,1)}) %reduce-scatter.4.cloned.1.call-update) | async-done | bytes 638992 | tf_op jit(solution)/shard_map/reduce_scatter | solution.py:92
  175.0 0.8 slice.27
  175.8 8.8 %psum.15 = bf16[48,512]{1,0:T(8,128)(2,1)S(1)} all-reduce(bf16[48,512]{1,0:T(8,128)(2,1)S(1)} %slice.27), channel_id=1, replica_groups=mesh['dp'=4,'row'=2,'col'=4] {'row'}, use_global_device_ids=true, to_apply=%region_6.7 | all-reduce | flops 24576 | bytes 98304 | tf_op jit(solution)/shard_map/psum | solution.py:34
  184.6 7.4 %fusion = bf16[48,6144]{1,0:T(8,128)(2,1)} fusion(bf16[48,512]{1,0:T(8,128)(2,1)S(1)} %psum.15, bf16[6144,512]{1,0:T(8,128)(2,1)} %bitcast.114, bf16[48,6656]{1,0:T(8,128)(2,1)} %reduce-scatter.4.cloned.1.call-done), kind=kOutput, calls=%fused_computation.8 | convolution fusion | flops 302874624 | bytes 7520256 | tf_op jit(solution)/shard_map/dot_general | solution.py:28
  192.0 44.0 %reduce-scatter.8.cloned.1.call-done = bf16[128,8,768]{2,0,1:T(8,128)(2,1)} async-done(((bf16[512,8,768]{2,0,1:T(8,128)(2,1)}), bf16[128,8,768]{2,0,1:T(8,128)(2,1)}) %reduce-scatter.8.cloned.1.call-update) | async-done | bytes 1572880 | tf_op jit(solution)/shard_map/reduce_scatter | solution.py:119
  235.9 4.1 %copy.64 = f32[128,8,768]{2,1,0:T(8,128)} copy(bf16[128,8,768]{2,0,1:T(8,128)(2,1)} %reduce-scatter.8.cloned.1.call-done) | data formatting | bytes 4718592
  240.0 76.3 %reduce-scatter.6.cloned.1.call-done = bf16[192,8,768]{2,1,0:T(8,128)(2,1)} async-done(((bf16[768,8,768]{2,1,0:T(8,128)(2,1)}), bf16[192,8,768]{2,1,0:T(8,128)(2,1)}) %reduce-scatter.6.cloned.1.call-update) | async-done | bytes 2359312 | tf_op jit(solution)/shard_map/reduce_scatter | solution.py:116
  316.4 4.2 %convert_element_type.58 = f32[192,8,768]{2,1,0:T(8,128)} convert(bf16[192,8,768]{2,1,0:T(8,128)(2,1)} %reduce-scatter.6.cloned.1.call-done) | non-fusion elementwise | flops 1179648 | bytes 7077888 | tf_op jit(solution)/shard_map/convert_element_type | solution.py:118
  (41 shorter events, 1.3 us)
Async XLA Ops:
  7.2 12.2 %copy-start = (bf16[96,6144]{1,0:T(8,128)(2,1)S(1)}, bf16[96,6144]{1,0:T(8,128)(2,1)}, u32[]{:S(2)}) copy-start(bf16[96,6144]{1,0:T(8,128)(2,1)} %param.8) | copy-start | bytes 3538948
  13.6 8.8 %all-to-all-start.1 = ((bf16[4,1,23]{2,1,0:T(2,128)(2,1)}), bf16[4,1,23]{2,1,0:T(2,128)(2,1)S(1)}, u32[]{:S(2)}, u32[]{:S(2)}) async-start(bf16[4,1,23]{2,1,0:T(2,128)(2,1)} %copy.55), calls=%async_computation.1 | async-start | bytes 4096 | tf_op jit(solution)/shard_map/all_to_all | solution.py:50
  22.4 19.3 %all-to-all-start = ((bf16[4,23,6144]{2,1,0:T(8,128)(2,1)}), bf16[4,23,6144]{2,1,0:T(8,128)(2,1)S(1)}, u32[]{:S(2)}, u32[]{:S(2)}) async-start(bf16[4,23,6144]{2,1,0:T(8,128)(2,1)} %broadcast_select_fusion), calls=%async_computation | async-start | bytes 2359296 | tf_op jit(solution)/shard_map/all_to_all | solution.py:49
  25.9 76.3 %all-gather.2.cloned.1.call-start = ((), (), s32[]{:S(2)}) async-start(), calls=%async_computation.5 | async-start | bytes 2949120 | tf_op jit(solution)/shard_map/all_gather | solution.py:68
  43.9 131.1 %reduce-scatter.4.cloned.1.call-start = ((), (), s32[]{:S(2)}) async-start(), calls=%async_computation.6 | async-start | bytes 3194880 | tf_op jit(solution)/shard_map/reduce_scatter | solution.py:92
  51.4 8.8 %copy-start.5 = (u32[32]{0:T(128)S(1)}, u32[32]{0:T(128)}, u32[]{:S(2)}) copy-start(u32[32]{0:T(128)} %constant.120) | copy-start | bytes 388
  51.4 23.4 %copy-start.2 = (bf16[48,6144]{1,0:T(8,128)(2,1)S(1)}, bf16[48,6144]{1,0:T(8,128)(2,1)}, u32[]{:S(2)}) copy-start(bf16[48,6144]{1,0:T(8,128)(2,1)} %broadcast_select_fusion.1) | copy-start | bytes 1769476
  102.2 6.6 %copy-start.4 = (bf16[192,8,768]{2,1,0:T(8,128)(2,1)S(1)}, bf16[192,8,768]{2,1,0:T(8,128)(2,1)}, u32[]{:S(2)}) copy-start(bf16[192,8,768]{2,1,0:T(8,128)(2,1)} %param.15) | copy-start | bytes 7077892
  102.2 14.5 %slice-start = ((s8[9437184]{0:T(1024)(128)(4,1)}), s8[4194304]{0:T(1024)(128)(4,1)S(1)}, s32[]{:S(2)}) async-start(s8[9437184]{0:T(1024)(128)(4,1)} %bitcast.111), calls=%async_computation.9 | async-start | bytes 8388608
  102.2 14.5 %slice-start.1 = ((s8[9437184]{0:T(1024)(128)(4,1)}), s8[4194304]{0:T(1024)(128)(4,1)S(1)}, s32[]{:S(2)}) async-start(s8[9437184]{0:T(1024)(128)(4,1)} %bitcast.111), calls=%async_computation.10 | async-start | bytes 8388608
  108.8 7.9 %slice-start.2 = ((s8[9437184]{0:T(1024)(128)(4,1)}), s8[1048576]{0:T(1024)(128)(4,1)S(1)}, s32[]{:S(2)}) async-start(s8[9437184]{0:T(1024)(128)(4,1)} %bitcast.111), calls=%async_computation.11 | async-start | bytes 2097152
  127.0 109.0 %reduce-scatter.8.cloned.1.call-start = ((), (), s32[]{:S(2)}) async-start(), calls=%async_computation.8 | async-start | bytes 7864320 | tf_op jit(solution)/shard_map/reduce_scatter | solution.py:119
  131.5 184.9 %reduce-scatter.6.cloned.1.call-start = ((), (), s32[]{:S(2)}) async-start(), calls=%async_computation.7 | async-start | bytes 11796480 | tf_op jit(solution)/shard_map/reduce_scatter | solution.py:116
  151.8 1.7 copy-start.3
  235.9 84.6 %copy-start.1 = (bf16[96,6144]{1,0:T(8,128)(2,1)S(1)}, bf16[96,6144]{1,0:T(8,128)(2,1)}, u32[]{:S(2)}) copy-start(bf16[96,6144]{1,0:T(8,128)(2,1)} %param.8) | copy-start | bytes 3538948
Sparse Core Ops, SparseCore 0:
  44.1 53.4 all-gather.1
  127.1 47.8 reduce-scatter.3
  177.5 58.3 reduce-scatter.7
  238.4 77.9 reduce-scatter.5
where the time goes:
time: 328 us; the launch traced here: 327 us
  waiting for transfers between devices  148 us (45%)
  local copies, waits for them, and re-layouts  47.1 us (14%)
  blocking collectives  45.3 us (14%)
  matrix products  45.3 us (14%)
  other arithmetic  18.6 us (6%)
  between operations  14.6 us (4%)
  starting transfers between devices  8.18 us (2%)
    reduce_scatter x1, waiting for transfers between devices, local(): lax.psum_scatter(block_term.astype(jnp.bfloat16), 'dp', scatter_dimension...  76.3 us
    reduce_scatter x1, waiting for transfers between devices, local(): lax.psum_scatter(out_term.astype(jnp.bfloat16), 'dp', scatter_dimension=0...  44 us
    reduce_scatter x1, waiting for transfers between devices, local(): lax.psum_scatter(jnp.concatenate([input_term.reshape(TOK_DEV * lax.axis_s...  18.9 us
    unnamed x24, local copies, waits for them, and re-layouts  16.7 us
    all_gather x1, blocking collectives, local(): lax.all_gather(own_low, 'col', axis=0, tiled=True)  14.8 us
    convert_element_type x1, local copies, waits for them, and re-layouts, local(): block_term.astype(jnp.bfloat16)  13.2 us
    unnamed x1, blocking collectives  13.1 us
    dot_general x2, matrix products, contract_last(): lax.dot_general(left_side, right_side, (((1,), (1,)), ((), ())), preferre...  12.4 us
  transfers between devices with their start and end apart: 6, of which 4 were waited for; matrix products, arithmetic and copies ran while one was open for 22% of the time, Pallas kernels for 0%

commit v1 on v0

v1 whole, which is shorter than its diff:
```python
import functools

import jax
import jax.numpy as jnp
from jax import lax
from jax.experimental import pallas as pl
from jax.experimental.pallas import tpu as pltpu
from jax.sharding import PartitionSpec as P

F32 = jnp.float32
BF16 = jnp.bfloat16


def dot(left, right, left_dim, right_dim):
    return lax.dot_general(
        left, right, (((left_dim,), (right_dim,)), ((), ())), preferred_element_type=F32
    )


def block_kernel(rows, weight, low, low_out, cot, tok_weight, act, grad, in_term, low_term):
    pre = dot(rows[...], weight[0], 1, 0) + dot(low[...], low_out[0], 1, 0)
    square = pre * pre
    tanh_val = jnp.tanh(0.7978845608 * (pre + 0.044715 * (square * pre)))
    half = 0.5 * (1.0 + tanh_val)
    act[0] = (pre * half).astype(BF16)
    slope = half + 0.5 * pre * (1.0 - tanh_val * tanh_val) * 0.7978845608 * (
        1.0 + 0.134145 * square
    )
    grad_pre = (tok_weight[...] * cot[0].astype(F32) * slope).astype(BF16)
    grad[0] = grad_pre
    in_term[...] = dot(grad_pre, weight[0], 1, 1).astype(BF16)
    part = dot(grad_pre, low_out[0], 1, 1)

    @pl.when(pl.program_id(0) == 0)
    def _():
        low_term[...] = part

    @pl.when(pl.program_id(0) > 0)
    def _():
        low_term[...] += part


def block_chunk(rows, row_base, weight, low, low_out, cot, tok_weight, base, count):
    tokens = rows.shape[0]
    n_blocks, width_in, width_out = weight.shape
    rank = low.shape[1]
    return pl.pallas_call(
        block_kernel,
        grid=(count,),
        in_specs=[
            pl.BlockSpec((tokens, width_in), lambda b: (0, row_base + b)),
            pl.BlockSpec((1, width_in, width_out), lambda b: (base + b, 0, 0)),
            pl.BlockSpec((tokens, rank), lambda b: (0, 0)),
            pl.BlockSpec((1, rank, width_out), lambda b: (base + b, 0, 0)),
            pl.BlockSpec((1, tokens, width_out), lambda b: (base + b, 0, 0)),
            pl.BlockSpec((tokens, 1), lambda b: (0, 0)),
        ],
        out_specs=[
            pl.BlockSpec((1, tokens, width_out), lambda b: (b, 0, 0)),
            pl.BlockSpec((1, tokens, width_out), lambda b: (b, 0, 0)),
            pl.BlockSpec((tokens, width_in), lambda b: (0, b)),
            pl.BlockSpec((tokens, rank), lambda b: (0, 0)),
        ],
        out_shape=[
            jax.ShapeDtypeStruct((count, tokens, width_out), BF16),
            jax.ShapeDtypeStruct((count, tokens, width_out), BF16),
            jax.ShapeDtypeStruct((tokens, count * width_in), BF16),
            jax.ShapeDtypeStruct((tokens, rank), F32),
        ],
        cost_estimate=pl.CostEstimate(
            flops=4 * count * tokens * width_out * (width_in + rank),
            bytes_accessed=2 * count * width_out * (width_in + rank + 3 * tokens),
            transcendentals=count * tokens * width_out,
        ),
    )(rows, weight, low, low_out, cot, tok_weight)


def split_kernel(n_parts, rows, out):
    part = out.shape[3]
    value = rows[...]
    for e in range(n_parts):
        out[e, 0] = value[:, e * part : (e + 1) * part]


def split_rows(rows, n_blocks, n_parts):
    tokens, width = rows.shape
    block_in = width // n_blocks
    part = block_in // n_parts
    return pl.pallas_call(
        functools.partial(split_kernel, n_parts),
        grid=(n_blocks,),
        in_specs=[pl.BlockSpec((tokens, block_in), lambda b: (0, b))],
        out_specs=pl.BlockSpec((n_parts, 1, tokens, part), lambda b: (0, b, 0, 0)),
        out_shape=jax.ShapeDtypeStruct((n_parts, n_blocks, tokens, part), BF16),
        cost_estimate=pl.CostEstimate(
            flops=0, bytes_accessed=4 * tokens * width, transcendentals=0
        ),
    )(rows)


def weight_kernel(n_groups, halves, chunks, *refs):
    rows = refs[: n_groups * halves]
    refs = refs[n_groups * halves :]
    lows = refs[:n_groups]
    grads = refs[n_groups : n_groups + n_groups * chunks]
    block_out, low_out = refs[n_groups + n_groups * chunks :]
    n_blocks = block_out.shape[1]
    per_chunk = n_blocks // chunks
    per_half = n_blocks // halves
    for b in range(n_blocks):
        block_sum = None
        low_sum = None
        for g in range(n_groups):
            grad = grads[g * chunks + b // per_chunk][b % per_chunk]
            row = rows[g * halves + b // per_half][b % per_half]
            block_part = dot(row, grad, 0, 0)
            low_part = dot(lows[g][...], grad, 0, 0)
            block_sum = block_part if g == 0 else block_sum + block_part
            low_sum = low_part if g == 0 else low_sum + low_part
        block_out[:, b, :] = block_sum
        low_out[:, b, :] = low_sum


def weight_grads(rows, lows, grads):
    n_groups = len(rows)
    halves = len(rows[0])
    chunks = len(grads[0])
    per_half, tokens, part = rows[0][0].shape
    per_chunk, _, width = grads[0][0].shape
    n_blocks = per_chunk * chunks
    rank = lows[0].shape[1]
    tile = 256 if width % 256 == 0 else width
    flat_rows = [x for group in rows for x in group]
    flat_grads = [x for group in grads for x in group]
    return pl.pallas_call(
        functools.partial(weight_kernel, n_groups, halves, chunks),
        grid=(width // tile,),
        in_specs=[pl.BlockSpec((per_half, tokens, part), lambda j: (0, 0, 0))] * len(flat_rows)
        + [pl.BlockSpec((tokens, rank), lambda j: (0, 0))] * n_groups
        + [pl.BlockSpec((per_chunk, tokens, tile), lambda j: (0, 0, j))] * len(flat_grads),
        out_specs=[
            pl.BlockSpec((part, n_blocks, tile), lambda j: (0, 0, j)),
            pl.BlockSpec((rank, n_blocks, tile), lambda j: (0, 0, j)),
        ],
        out_shape=[
            jax.ShapeDtypeStruct((part, n_blocks, width), F32),
            jax.ShapeDtypeStruct((rank, n_blocks, width), F32),
        ],
        cost_estimate=pl.CostEstimate(
            flops=2 * n_groups * tokens * n_blocks * width * (part + rank),
            bytes_accessed=2 * n_groups * tokens * n_blocks * width
            + 4 * (part + rank) * n_blocks * width,
            transcendentals=0,
        ),
    )(*flat_rows, *lows, *flat_grads)


def doc_weights(segment_row, alive_count):
    slot_ids = jnp.arange(segment_row.shape[0], dtype=jnp.int32)
    is_alive = slot_ids < alive_count
    same_doc = (segment_row[:, None] == segment_row[None, :]) & is_alive[None, :]
    doc_length = jnp.sum(same_doc.astype(F32), axis=1)
    return (32.0 / (16.0 + doc_length)).astype(BF16)


def swap(value, axis, mask):
    return lax.ppermute(value, axis, [(s, s ^ mask) for s in range(lax.axis_size(axis))])


def row_total(partial_sum):
    mine = partial_sum.astype(BF16)
    if lax.axis_size("row") == 2:
        return mine.astype(F32) + swap(mine, "row", 1).astype(F32)
    return lax.psum(mine, "row").astype(F32)


def gather_groups(value, masks):
    held = [value]
    for mask in masks:
        held = held + [swap(x, "dp", mask) for x in held]
    return held


def local(
    source_rows, segments, send_slots, send_counts, block_weight, lowrank_in, lowrank_out, cotangent
):
    n_data = lax.axis_size("dp")
    n_col = lax.axis_size("col")
    my_data = lax.axis_index("dp")
    n_blocks, block_in, block_out = block_weight.shape
    rank_width = lowrank_in.shape[2]
    group_rows = cotangent.shape[0]
    own_rows = group_rows // n_col
    count_table = send_counts[0]
    slot_table = send_slots[0]
    outgoing = jnp.take(source_rows, slot_table, axis=0)
    incoming = lax.all_to_all(outgoing, "dp", split_axis=0, concat_axis=0, tiled=True)
    capacity = slot_table.shape[1]
    arrivals = lax.dynamic_index_in_dim(count_table, my_data, 1, keepdims=False)
    starts = jnp.cumsum(arrivals) - arrivals
    positions = jnp.arange(own_rows, dtype=jnp.int32)
    sender = jnp.sum((starts[None, :] <= positions[:, None]).astype(jnp.int32), axis=1) - 1
    offset = positions - jnp.take(starts, sender)
    flat_index = sender * capacity + offset
    my_rows = jnp.take(incoming.reshape(n_data * capacity, incoming.shape[2]), flat_index, axis=0)

    segment_row, _ = lax.optimization_barrier((segments[0], outgoing))
    my_alive = jnp.sum(lax.dynamic_index_in_dim(count_table, my_data, 0, keepdims=False))
    weights = doc_weights(segment_row, my_alive)
    out_weights = jnp.take(weights, slot_table, axis=0)
    in_weights = lax.all_to_all(out_weights, "dp", split_axis=0, concat_axis=0, tiled=True)
    my_weights = jnp.take(in_weights.reshape(n_data * capacity), flat_index, axis=0)

    flat_in = lowrank_in.reshape(n_blocks * block_in, rank_width)
    own_part = jnp.dot(my_rows, flat_in, preferred_element_type=F32)
    own_low = row_total(own_part).astype(BF16)
    own_extra = jnp.concatenate(
        [own_low, jnp.broadcast_to(my_weights[:, None], (own_rows, 128))], axis=1
    )
    halves = 2
    half_width = n_blocks * block_in // halves
    panel_low = None
    panels = []
    for h in range(halves):
        piece = my_rows[:, h * half_width : (h + 1) * half_width]
        panels.append(lax.all_gather(piece, "col", axis=0, tiled=True))
        if h == 0:
            extra = lax.all_gather(own_extra, "col", axis=0, tiled=True)
            panel_low = extra[:, :rank_width]
            tok_weight = extra[:, rank_width : rank_width + 1].astype(F32)

    low_out_blocks = jnp.transpose(lowrank_out, (1, 0, 2))
    cot_blocks = jnp.transpose(cotangent, (1, 0, 2))

    masks = []
    bit = n_data // 2
    while bit:
        masks.append(bit)
        bit //= 2
    offsets = [0]
    for mask in masks:
        offsets = offsets + [k ^ mask for k in offsets]

    low_split = jnp.transpose(panel_low.reshape(group_rows, n_data, -1), (1, 0, 2))
    per_half = n_blocks // halves
    chunks = min(4, n_blocks)
    per_chunk = n_blocks // chunks
    acts, grads, in_terms, low_terms, row_parts = [], [], [], [], []
    for h in range(halves):
        row_parts.append(split_rows(panels[h], per_half, n_data))
    for c in range(chunks):
        h = c * per_chunk // per_half
        act, grad, in_term, low_term = block_chunk(
            panels[h],
            c * per_chunk - h * per_half,
            block_weight,
            panel_low,
            low_out_blocks,
            cot_blocks,
            tok_weight,
            c * per_chunk,
            per_chunk,
        )
        acts.append(act)
        grads.append(gather_groups(grad, masks))
        in_terms.append(in_term)
        low_terms.append(low_term)

    group_slices, group_lows = [], []
    for k in offsets:
        pieces = []
        for h in range(halves):
            piece = lax.dynamic_index_in_dim(row_parts[h], my_data ^ k, 0, keepdims=False)
            pieces.append(swap(piece, "dp", k) if k else piece)
        group_slices.append(pieces)
        low_piece = lax.dynamic_index_in_dim(low_split, my_data ^ k, 0, keepdims=False)
        group_lows.append(swap(low_piece, "dp", k) if k else low_piece)

    own_low_term = lax.psum_scatter(
        sum(low_terms).astype(BF16), "col", scatter_dimension=0, tiled=True
    )
    low_grad = row_total(own_low_term).astype(BF16)
    half_chunks = chunks // halves
    terms = []
    for h in range(halves):
        part = jnp.concatenate(in_terms[h * half_chunks : (h + 1) * half_chunks], axis=1)
        terms.append(lax.psum_scatter(part, "col", scatter_dimension=0, tiled=True))
    own_term = jnp.concatenate(terms, axis=1).astype(F32)
    input_grad = (own_term + dot(low_grad, flat_in, 1, 1)).astype(BF16)

    act_out = jnp.transpose(jnp.concatenate(acts, axis=0), (1, 0, 2))
    by_group = [[grads[c][g] for c in range(chunks)] for g in range(n_data)]
    block_grad, out_grad = weight_grads(group_slices, group_lows, by_group)
    return (act_out, input_grad, block_grad, out_grad)


def solution(mesh):
    in_specs = (
        P(("dp", "col"), "row"),
        P(("dp", "col"), None),
        P(("dp", "col"), None, None),
        P("col", None, None),
        P("row", None, "col"),
        P("row", None, None),
        P(None, "row", "col"),
        P("dp", "row", "col"),
    )
    out_specs = (
        P("dp", "row", "col"),
        P(("dp", "col"), "row"),
        P("dp", "row", "col"),
        P("dp", "row", "col"),
    )
    return jax.shard_map(local, mesh=mesh, in_specs=in_specs, out_specs=out_specs, check_vma=False)
```

time: 328 us -> 260 us (0.79)
  Pallas kernels: 0 us -> 43.7 us
  waiting for transfers between devices: 148 us -> 105 us
  matrix products: 45.3 us -> 9.67 us
  blocking collectives: 45.3 us -> 16.3 us
  local copies, waits for them, and re-layouts: 47.1 us -> 29.8 us
  starting transfers between devices: 8.18 us -> 24.7 us
    reduce_scatter x3, waiting for transfers between devices: 139 us -> 0.04 us  [the longest x2 0.04 us: local(): terms.append(lax.psum_scatter(part, 'col', scatter_dimension=0, tiled=True))]
    ppermute x0 -> x23, waiting for transfers between devices: none -> 70.9 us  [swap(): lax.ppermute(value, axis, [(s, s ^ mask) for s in range(lax.axis_size(axi...]
    pallas_call x0 -> x7, Pallas kernels: none -> 43.7 us  [the longest x4 24.5 us: block_chunk(): pl.pallas_call(block_kernel, grid=(count,), in_specs=[pl.BlockSpec((token...]
    dot_general x8 -> x2, matrix products: 45.3 us -> 9.67 us  [the longest x1 5.71 us: dot(): lax.dot_general(left, right, (((left_dim,), (right_dim,)), ((), ())), pre...]
    all_gather x1 -> x2, waiting for transfers between devices: 0.01 us -> 20.5 us  [local(): panels.append(lax.all_gather(piece, 'col', axis=0, tiled=True))]
    psum x2 -> x0, blocking collectives: 17.4 us -> none  [the longest x1 8.78 us: row_total(): return lax.psum(partial_sum.astype(jnp.bfloat16), 'row').astype(jnp.float32)]
    ppermute x0 -> x23, starting transfers between devices: none -> 16.5 us  [swap(): lax.ppermute(value, axis, [(s, s ^ mask) for s in range(lax.axis_size(axi...]
    convert_element_type x1 -> x0, local copies, waits for them, and re-layouts: 13.2 us -> none  [local(): block_term.astype(jnp.bfloat16)]
  transfers between devices with their start and end apart: 6 -> 30, of which waited for: 4 -> 10; matrix products, arithmetic and copies ran while one was open for 22% -> 14% of each run, Pallas kernels for 0% -> 12%
where the time goes in v1:
time: 260 us; the launch traced here: 259 us
  waiting for transfers between devices  105 us (40%)
  Pallas kernels  43.7 us (17%)
  local copies, waits for them, and re-layouts  29.8 us (11%)
  starting transfers between devices  24.7 us (10%)
  blocking collectives  16.3 us (6%)
  other arithmetic  15.8 us (6%)
  between operations  14.3 us (6%)
  matrix products  9.67 us (4%)
    ppermute x23, waiting for transfers between devices, swap(): lax.ppermute(value, axis, [(s, s ^ mask) for s in range(lax.axis_size(axi...  70.9 us
    pallas_call x4, Pallas kernels, block_chunk(): pl.pallas_call(block_kernel, grid=(count,), in_specs=[pl.BlockSpec((token...  24.5 us
    all_gather x2, waiting for transfers between devices, local(): panels.append(lax.all_gather(piece, 'col', axis=0, tiled=True))  20.5 us
    ppermute x23, starting transfers between devices, swap(): lax.ppermute(value, axis, [(s, s ^ mask) for s in range(lax.axis_size(axi...  16.5 us
    all_gather x1, blocking collectives, local(): extra = lax.all_gather(own_extra, 'col', axis=0, tiled=True)  16.3 us
    unnamed x75, local copies, waits for them, and re-layouts  15.6 us
    pallas_call x1, Pallas kernels, weight_grads(): pl.pallas_call(functools.partial(weight_kernel, n_groups, halves, chunks)...  11.7 us
    all_to_all x1, waiting for transfers between devices, local(): lax.all_to_all(outgoing, 'dp', split_axis=0, concat_axis=0, tiled=True)  9.14 us
  transfers between devices with their start and end apart: 30, of which 10 were waited for; matrix products, arithmetic and copies ran while one was open for 14% of the time, Pallas kernels for 12%

profile of v1, /device:TPU:0, one launch (start us, length us, event | category | flops | bytes accessed | tf_op | source)
XLA Modules:
  0.0 259.1 jit_solution(8202186060494078889)
XLA Ops:
  7.2 0.8 compare_select_fusion.1
  8.7 1.2 gather_fusion
  10.4 1.2 broadcast_select_fusion
  13.1 1.2 gather_fusion.2
  15.0 4.3 %all-to-all-start.1 = ((bf16[4,1,23]{2,1,0:T(2,128)(2,1)}), bf16[4,1,23]{2,1,0:T(2,128)(2,1)S(1)}, u32[]{:S(2)}, u32[]{:S(2)}) async-start(bf16[4,1,23]{2,1,0:T(2,128)(2,1)} %copy.42), calls=%async_computation.1 | async-start | bytes 4096 | tf_op jit(solution)/shard_map/all_to_all | solution.py:211
  19.6 3.3 %all-to-all-done.1 = bf16[4,1,23]{2,1,0:T(2,128)(2,1)S(1)} async-done(((bf16[4,1,23]{2,1,0:T(2,128)(2,1)}), bf16[4,1,23]{2,1,0:T(2,128)(2,1)S(1)}, u32[]{:S(2)}, u32[]{:S(2)}) %all-to-all-start.1) | async-done | bytes 216 | tf_op jit(solution)/shard_map/all_to_all | solution.py:211
  23.0 3.5 %all-to-all-start = ((bf16[4,23,6144]{2,1,0:T(8,128)(2,1)}), bf16[4,23,6144]{2,1,0:T(8,128)(2,1)S(1)}, u32[]{:S(2)}, u32[]{:S(2)}) async-start(bf16[4,23,6144]{2,1,0:T(8,128)(2,1)} %broadcast_select_fusion), calls=%async_computation | async-start | bytes 2359296 | tf_op jit(solution)/shard_map/all_to_all | solution.py:197
  27.2 2.5 fusion.4
  30.7 2.5 broadcast_select_fusion.2
  33.2 9.1 %all-to-all-done = bf16[4,23,6144]{2,1,0:T(8,128)(2,1)S(1)} async-done(((bf16[4,23,6144]{2,1,0:T(8,128)(2,1)}), bf16[4,23,6144]{2,1,0:T(8,128)(2,1)S(1)}, u32[]{:S(2)}, u32[]{:S(2)}) %all-to-all-start) | async-done | bytes 1130528 | tf_op jit(solution)/shard_map/all_to_all | solution.py:197
  42.7 0.9 gather_fusion.1
  43.7 0.8 fusion.7
  45.4 4.0 %convolution_convert_fusion = bf16[48,512]{1,0:T(8,128)(2,1)S(1)} fusion(bf16[48,6144]{1,0:T(8,128)(2,1)S(1)} %broadcast_select_fusion.1, bf16[6144,512]{1,0:T(8,128)(2,1)} %bitcast.102), kind=kOutput, calls=%fused_computation.12 | convolution fusion | flops 302014464 | bytes 6930432 | tf_op jit(solution)/shard_map/dot_general | solution.py:215
  49.3 2.0 collective-permute-start
  51.3 7.1 %copy.60 = bf16[512,8,768]{2,0,1:T(8,128)(2,1)} copy(bf16[512,8,768]{2,1,0:T(8,128)(2,1)} %param.14) | data formatting | bytes 12582912 | tf_op args[6]
  58.4 1.9 copy.61
  60.4 16.3 %all_gather.10 = bf16[192,640]{1,0:T(8,128)(2,1)S(1)} all-gather(bf16[48,640]{1,0:T(8,128)(2,1)S(1)} %pad_maximum_fusion.2), channel_id=1, replica_groups=mesh['dp'=4,'row'=2,'col'=4] {'col'}, dimensions={0}, use_global_device_ids=true | all-gather | bytes 307200 | tf_op jit(solution)/shard_map/all_gather | solution.py:228
  78.0 1.6 all-gather.5.cloned.1.call-done.rows
  79.6 6.0 %shard_map.114 = (bf16[2,192,768]{2,1,0:T(8,128)(2,1)}, bf16[2,192,768]{2,1,0:T(8,128)(2,1)}, bf16[192,1536]{1,0:T(8,128)(2,1)}, f32[192,512]{1,0:T(8,128)}) custom-call(bf16[192,3072]{1,0:T(8,128)(2,1)} %all-gather.5.cloned.1.call-done.rows, bf16[8,768,768]{2,1,0:T(8,128)(2,1)} %weight.7, bf16[192,512]{1,0:T(8,128)(2,1)} %slice.30.low, ...), custom_call_target="tpu_custom_call" | custom-call | flops 1509949440 | bytes 5701632 | tf_op jit(solution)/shard_map/pallas_call | solution.py:47
  85.7 6.2 %shard_map.113 = (bf16[2,192,768]{2,1,0:T(8,128)(2,1)}, bf16[2,192,768]{2,1,0:T(8,128)(2,1)}, bf16[192,1536]{1,0:T(8,128)(2,1)}, f32[192,512]{1,0:T(8,128)}) custom-call(bf16[192,3072]{1,0:T(8,128)(2,1)} %all-gather.5.cloned.1.call-done.rows, bf16[8,768,768]{2,1,0:T(8,128)(2,1)} %weight.7, bf16[192,512]{1,0:T(8,128)(2,1)} %slice.30.low, ...), custom_call_target="tpu_custom_call" | custom-call | flops 1509949440 | bytes 5701632 | tf_op jit(solution)/shard_map/pallas_call | solution.py:47
  91.9 18.8 %all-gather.3.cloned.1.call-done.rows = bf16[192,3072]{1,0:T(8,128)(2,1)} async-done(((bf16[48,3072]{1,0:T(8,128)(2,1)}), bf16[192,3072]{1,0:T(8,128)(2,1)}) %all-gather.3.cloned.1.call-update) | async-done | bytes 1179664 | tf_op jit(solution)/shard_map/all_gather | solution.py:226
  110.7 6.1 %shard_map.112 = (bf16[2,192,768]{2,1,0:T(8,128)(2,1)}, bf16[2,192,768]{2,1,0:T(8,128)(2,1)}, bf16[192,1536]{1,0:T(8,128)(2,1)}, f32[192,512]{1,0:T(8,128)}) custom-call(bf16[192,3072]{1,0:T(8,128)(2,1)} %all-gather.3.cloned.1.call-done.rows, bf16[8,768,768]{2,1,0:T(8,128)(2,1)} %weight.7, bf16[192,512]{1,0:T(8,128)(2,1)} %slice.30.low, ...), custom_call_target="tpu_custom_call" | custom-call | flops 1509949440 | bytes 5701632 | tf_op jit(solution)/shard_map/pallas_call | solution.py:47
  116.9 6.2 %shard_map.111 = (bf16[2,192,768]{2,1,0:T(8,128)(2,1)}, bf16[2,192,768]{2,1,0:T(8,128)(2,1)}, bf16[192,1536]{1,0:T(8,128)(2,1)}, f32[192,512]{1,0:T(8,128)}) custom-call(bf16[192,3072]{1,0:T(8,128)(2,1)} %all-gather.3.cloned.1.call-done.rows, bf16[8,768,768]{2,1,0:T(8,128)(2,1)} %weight.7, bf16[192,512]{1,0:T(8,128)(2,1)} %slice.30.low, ...), custom_call_target="tpu_custom_call" | custom-call | flops 1509949440 | bytes 5701632 | tf_op jit(solution)/shard_map/pallas_call | solution.py:47
  123.1 1.9 add_convert_fusion
  125.1 1.2 pad_maximum_fusion.1
  126.9 1.2 pad_maximum_fusion
  128.1 1.1 constant_dynamic-slice_fusion
  129.8 1.5 collective-permute-start.8
  133.1 3.7 %shard_map.115 = bf16[4,4,192,192]{3,2,1,0:T(8,128)(2,1)} custom-call(bf16[192,3072]{1,0:T(8,128)(2,1)} %all-gather.3.cloned.1.call-done.rows), custom_call_target="tpu_custom_call" | custom-call | bytes 2359296 | tf_op jit(solution)/shard_map/pallas_call | solution.py:89
  136.9 2.6 dynamic-slice_bitcast_fusion.1
  139.4 1.5 collective-permute-start.2
  140.9 3.8 %shard_map.116 = bf16[4,4,192,192]{3,2,1,0:T(8,128)(2,1)} custom-call(bf16[192,3072]{1,0:T(8,128)(2,1)} %all-gather.5.cloned.1.call-done.rows), custom_call_target="tpu_custom_call" | custom-call | bytes 2359296 | tf_op jit(solution)/shard_map/pallas_call | solution.py:89
  144.7 2.4 dynamic-slice_bitcast_fusion
  147.7 1.5 collective-permute-start.11
  149.8 1.9 collective-permute-done.2.refs_2_
  151.7 8.3 %collective-permute-done.3.refs_3_ = bf16[4,192,192]{2,1,0:T(8,128)(2,1)S(1)} collective-permute-done((bf16[4,192,192]{2,1,0:T(8,128)(2,1)S(1)}, bf16[4,192,192]{2,1,0:T(8,128)(2,1)S(1)}, u32[]{:S(2)}, u32[]{:S(2)}) %collective-permute-start.3) | collective-permute-done | bytes 294944 | tf_op jit(solution)/shard_map/ppermute | solution.py:167
  160.1 1.7 collective-permute-start.7
  161.8 1.5 collective-permute-start.13
  163.3 29.5 %collective-permute-done.6.refs_6_ = bf16[4,192,192]{2,1,0:T(8,128)(2,1)S(1)} collective-permute-done((bf16[4,192,192]{2,1,0:T(8,128)(2,1)}, bf16[4,192,192]{2,1,0:T(8,128)(2,1)S(1)}, u32[]{:S(2)}, u32[]{:S(2)}) %collective-permute-start.6) | collective-permute-done | bytes 294944 | tf_op jit(solution)/shard_map/ppermute | solution.py:167
  193.4 7.7 %collective-permute-done.7.refs_7_ = bf16[4,192,192]{2,1,0:T(8,128)(2,1)S(1)} collective-permute-done((bf16[4,192,192]{2,1,0:T(8,128)(2,1)S(1)}, bf16[4,192,192]{2,1,0:T(8,128)(2,1)S(1)}, u32[]{:S(2)}, u32[]{:S(2)}) %collective-permute-start.7) | collective-permute-done | bytes 294944 | tf_op jit(solution)/shard_map/ppermute | solution.py:167
  201.2 1.2 collective-permute-start.15
  203.2 11.7 %collective-permute-done.13.refs_18_ = bf16[2,192,768]{2,1,0:T(8,128)(2,1)} collective-permute-done((bf16[2,192,768]{2,1,0:T(8,128)(2,1)S(1)}, bf16[2,192,768]{2,1,0:T(8,128)(2,1)}, u32[]{:S(2)}, u32[]{:S(2)}) %collective-permute-start.13) | collective-permute-done | bytes 589856 | tf_op jit(solution)/shard_map/ppermute | solution.py:167
  214.9 11.7 %collective-permute-done.14.refs_19_ = bf16[2,192,768]{2,1,0:T(8,128)(2,1)} collective-permute-done((bf16[2,192,768]{2,1,0:T(8,128)(2,1)S(1)}, bf16[2,192,768]{2,1,0:T(8,128)(2,1)}, u32[]{:S(2)}, u32[]{:S(2)}) %collective-permute-start.14) | collective-permute-done | bytes 589856 | tf_op jit(solution)/shard_map/ppermute | solution.py:167
  228.3 1.4 maximum_bitcast_fusion
  229.7 2.7 %copy.49 = bf16[192,8,768]{2,1,0:T(8,128)(2,1)} copy(bf16[192,8,768]{2,0,1:T(8,128)(2,1)S(1)} %maximum_bitcast_fusion) | data formatting | bytes 4718592
  232.4 1.5 collective-permute-start.1
  235.1 11.7 %shard_map.117 = (f32[192,8,768]{2,1,0:T(8,128)}, f32[128,8,768]{2,1,0:T(8,128)}) custom-call(bf16[4,192,192]{2,1,0:T(8,128)(2,1)} %get-tuple-element.71.refs_0_, bf16[4,192,192]{2,1,0:T(8,128)(2,1)} %get-tuple-element.67.refs_1_, bf16[4,192,192]{2,1,0:T(8,128)(2,1)} %collective-permute-done.2.refs_2_, bf16[4,192,192]{2,1,0:T(8,128)(2,1)} %copy-done.21, ...), custom_call_target="tpu_custom_call" | custom-call | flops 3019898880 | bytes 17301504 | tf_op jit(solution)/shard_map/pallas_call | solution.py:135
  246.8 5.7 %fusion = bf16[48,6144]{1,0:T(8,128)(2,1)} fusion(bf16[6144,512]{1,0:T(8,128)(2,1)} %bitcast.103, bf16[48,3072]{1,0:T(8,128)(2,1)} %reduce-scatter.6.cloned.1.call-done, bf16[48,3072]{1,0:T(8,128)(2,1)} %reduce-scatter.4.cloned.1.call-done, bf16[48,512]{1,0:T(8,128)(2,1)S(1)} %collective-permute-done.1, bf16[48,512]{1,0:T(8,128)(2,1)S(1)} %copy-done.30), kind=kOutput, calls=%fused_computation.5 | convolution fusion | flops 303857664 | bytes 7569408 | tf_op jit(solution)/shard_map/dot_general | solution.py:15
  (145 shorter events, 16.6 us)
Async XLA Ops:
  10.4 4.0 %copy-start.31 = (s32[1,4,23]{2,1,0:T(4,128)S(1)}, s32[1,4,23]{2,1,0:T(4,128)}, u32[]{:S(2)}) copy-start(s32[1,4,23]{2,1,0:T(4,128)} %param.10) | copy-start | bytes 1108
  15.0 8.0 %all-to-all-start.1 = ((bf16[4,1,23]{2,1,0:T(2,128)(2,1)}), bf16[4,1,23]{2,1,0:T(2,128)(2,1)S(1)}, u32[]{:S(2)}, u32[]{:S(2)}) async-start(bf16[4,1,23]{2,1,0:T(2,128)(2,1)} %copy.42), calls=%async_computation.1 | async-start | bytes 4096 | tf_op jit(solution)/shard_map/all_to_all | solution.py:211
  23.0 19.3 %all-to-all-start = ((bf16[4,23,6144]{2,1,0:T(8,128)(2,1)}), bf16[4,23,6144]{2,1,0:T(8,128)(2,1)S(1)}, u32[]{:S(2)}, u32[]{:S(2)}) async-start(bf16[4,23,6144]{2,1,0:T(8,128)(2,1)} %broadcast_select_fusion), calls=%async_computation | async-start | bytes 2359296 | tf_op jit(solution)/shard_map/all_to_all | solution.py:197
  26.5 53.1 %all-gather.5.cloned.1.call-start = ((), (), s32[]{:S(2)}) async-start(), calls=%async_computation.6 | async-start | bytes 1474560 | tf_op jit(solution)/shard_map/all_gather | solution.py:226
  44.6 66.2 %all-gather.3.cloned.1.call-start = ((), (), s32[]{:S(2)}) async-start(), calls=%async_computation.5 | async-start | bytes 1474560 | tf_op jit(solution)/shard_map/all_gather | solution.py:226
  45.3 187.1 %reduce-scatter.8.cloned.1.call-start = ((), (), s32[]{:S(2)}) async-start(), calls=%async_computation.9 | async-start | bytes 245760 | tf_op jit(solution)/shard_map/reduce_scatter | solution.py:279
  49.3 10.9 %collective-permute-start = (bf16[48,512]{1,0:T(8,128)(2,1)S(1)}, bf16[48,512]{1,0:T(8,128)(2,1)S(1)}, u32[]{:S(2)}, u32[]{:S(2)}) collective-permute-start(bf16[48,512]{1,0:T(8,128)(2,1)S(1)} %convolution_convert_fusion), channel_id=1, source_target_pairs={{0,4},{4,0},{1,5},{5,1},{2,6},{6,2},{3,7},{7,3},{8,12},{12,8},{9,1... | collective-permute-start | bytes 147464 | tf_op jit(solution)/shard_map/ppermute | solution.py:167
  51.3 7.1 %copy-start.3 = (bf16[192,8,768]{2,1,0:T(8,128)(2,1)S(1)}, bf16[192,8,768]{2,1,0:T(8,128)(2,1)}, u32[]{:S(2)}) copy-start(bf16[192,8,768]{2,1,0:T(8,128)(2,1)} %param.15) | copy-start | bytes 7077892
  116.9 6.2 %copy-start.26 = (f32[192,512]{1,0:T(8,128)S(1)}, f32[192,512]{1,0:T(8,128)}, u32[]{:S(2)}) copy-start(f32[192,512]{1,0:T(8,128)} %get-tuple-element.35) | copy-start | bytes 1179652
  116.9 6.2 %copy-start.27 = (f32[192,512]{1,0:T(8,128)S(1)}, f32[192,512]{1,0:T(8,128)}, u32[]{:S(2)}) copy-start(f32[192,512]{1,0:T(8,128)} %get-tuple-element.34) | copy-start | bytes 1179652
  116.9 6.2 %copy-start.28 = (f32[192,512]{1,0:T(8,128)S(1)}, f32[192,512]{1,0:T(8,128)}, u32[]{:S(2)}) copy-start(f32[192,512]{1,0:T(8,128)} %get-tuple-element.33) | copy-start | bytes 1179652
  125.0 121.7 %reduce-scatter.6.cloned.1.call-start = ((), (), s32[]{:S(2)}) async-start(), calls=%async_computation.8 | async-start | bytes 1474560 | tf_op jit(solution)/shard_map/reduce_scatter | solution.py:287
  126.3 120.5 %reduce-scatter.4.cloned.1.call-start = ((), (), s32[]{:S(2)}) async-start(), calls=%async_computation.7 | async-start | bytes 1474560 | tf_op jit(solution)/shard_map/reduce_scatter | solution.py:287
  129.8 17.9 %collective-permute-start.8 = (bf16[192,128]{1,0:T(8,128)(2,1)}, bf16[192,128]{1,0:T(8,128)(2,1)}, u32[]{:S(2)}, u32[]{:S(2)}) collective-permute-start(bf16[192,128]{1,0:T(8,128)(2,1)} %bitcast.92), channel_id=1, source_target_pairs={{0,16},{8,24},{16,0},{24,8},{1,17},{9,25},{17,1},{25,9},{2,18},{10... | collective-permute-start | bytes 147464 | tf_op jit(solution)/shard_map/ppermute | solution.py:167
  131.8 15.9 %collective-permute-start.9 = (bf16[192,128]{1,0:T(8,128)(2,1)}, bf16[192,128]{1,0:T(8,128)(2,1)}, u32[]{:S(2)}, u32[]{:S(2)}) collective-permute-start(bf16[192,128]{1,0:T(8,128)(2,1)} %bitcast.91), channel_id=1, source_target_pairs={{0,8},{8,0},{16,24},{24,16},{1,9},{9,1},{17,25},{25,17},{2,10},{10... | collective-permute-start | bytes 147464 | tf_op jit(solution)/shard_map/ppermute | solution.py:167
  132.5 16.8 %collective-permute-start.10 = (bf16[192,128]{1,0:T(8,128)(2,1)}, bf16[192,128]{1,0:T(8,128)(2,1)}, u32[]{:S(2)}, u32[]{:S(2)}) collective-permute-start(bf16[192,128]{1,0:T(8,128)(2,1)} %bitcast.90), channel_id=1, source_target_pairs={{0,24},{8,16},{16,8},{24,0},{1,25},{9,17},{17,9},{25,1},{2,26},{10... | collective-permute-start | bytes 147464 | tf_op jit(solution)/shard_map/ppermute | solution.py:167
  139.4 12.3 %collective-permute-start.2 = (bf16[4,192,192]{2,1,0:T(8,128)(2,1)}, bf16[4,192,192]{2,1,0:T(8,128)(2,1)}, u32[]{:S(2)}, u32[]{:S(2)}) collective-permute-start(bf16[4,192,192]{2,1,0:T(8,128)(2,1)} %get-tuple-element.70), channel_id=1, source_target_pairs={{0,16},{8,24},{16,0},{24,8},{1,17},{9,25},{17,1},{25,9},{2,18},{10... | collective-permute-start | bytes 884744 | tf_op jit(solution)/shard_map/ppermute | solution.py:167
  140.9 87.4 %copy-start.9 = (bf16[2,192,768]{2,1,0:T(8,128)(2,1)S(1)}, bf16[2,192,768]{2,1,0:T(8,128)(2,1)}, u32[]{:S(2)}) copy-start(bf16[2,192,768]{2,1,0:T(8,128)(2,1)} %get-tuple-element.26) | copy-start | bytes 1769476
  140.9 87.4 %copy-start.10 = (bf16[2,192,768]{2,1,0:T(8,128)(2,1)S(1)}, bf16[2,192,768]{2,1,0:T(8,128)(2,1)}, u32[]{:S(2)}) copy-start(bf16[2,192,768]{2,1,0:T(8,128)(2,1)} %get-tuple-element.25) | copy-start | bytes 1769476
  144.7 4.6 %copy-start.6 = (bf16[2,192,768]{2,1,0:T(8,128)(2,1)S(1)}, bf16[2,192,768]{2,1,0:T(8,128)(2,1)}, u32[]{:S(2)}) copy-start(bf16[2,192,768]{2,1,0:T(8,128)(2,1)} %get-tuple-element.37.refs_13_) | copy-start | bytes 1769476
  144.7 17.1 %copy-start.5 = (bf16[2,192,768]{2,1,0:T(8,128)(2,1)S(1)}, bf16[2,192,768]{2,1,0:T(8,128)(2,1)}, u32[]{:S(2)}) copy-start(bf16[2,192,768]{2,1,0:T(8,128)(2,1)} %get-tuple-element.38.refs_14_) | copy-start | bytes 1769476
  144.7 48.1 %copy-start.4 = (bf16[2,192,768]{2,1,0:T(8,128)(2,1)S(1)}, bf16[2,192,768]{2,1,0:T(8,128)(2,1)}, u32[]{:S(2)}) copy-start(bf16[2,192,768]{2,1,0:T(8,128)(2,1)} %get-tuple-element.39.refs_15_) | copy-start | bytes 1769476
  144.7 82.9 %copy-start.29 = (bf16[192,1,128]{2,1,0:T(2,128)(2,1)S(1)}, bf16[192,1,128]{2,1,0:T(2,128)(2,1)}, u32[]{:S(2)}) copy-start(bf16[192,1,128]{2,1,0:T(2,128)(2,1)} %get-tuple-element.77) | copy-start | bytes 147460
  144.7 83.5 %copy-start.8 = (bf16[2,192,768]{2,1,0:T(8,128)(2,1)S(1)}, bf16[2,192,768]{2,1,0:T(8,128)(2,1)}, u32[]{:S(2)}) copy-start(bf16[2,192,768]{2,1,0:T(8,128)(2,1)} %get-tuple-element.27) | copy-start | bytes 1769476
  147.1 12.9 %collective-permute-start.3 = (bf16[4,192,192]{2,1,0:T(8,128)(2,1)S(1)}, bf16[4,192,192]{2,1,0:T(8,128)(2,1)S(1)}, u32[]{:S(2)}, u32[]{:S(2)}) collective-permute-start(bf16[4,192,192]{2,1,0:T(8,128)(2,1)S(1)} %get-tuple-element.66), channel_id=1, source_target_pairs={{0,16},{8,24},{16,0},{24,8},{1,17},{9,25},{17,1},{25,9},{2,18},{10... | collective-permute-start | bytes 884744 | tf_op jit(solution)/shard_map/ppermute | solution.py:167
  147.7 12.3 %collective-permute-start.4 = (bf16[4,192,192]{2,1,0:T(8,128)(2,1)}, bf16[4,192,192]{2,1,0:T(8,128)(2,1)S(1)}, u32[]{:S(2)}, u32[]{:S(2)}) collective-permute-start(bf16[4,192,192]{2,1,0:T(8,128)(2,1)} %get-tuple-element.69), channel_id=1, source_target_pairs={{0,8},{8,0},{16,24},{24,16},{1,9},{9,1},{17,25},{25,17},{2,10},{10... | collective-permute-start | bytes 884744 | tf_op jit(solution)/shard_map/ppermute | solution.py:167
  147.7 54.7 %collective-permute-start.11 = (bf16[2,192,768]{2,1,0:T(8,128)(2,1)S(1)}, bf16[2,192,768]{2,1,0:T(8,128)(2,1)}, u32[]{:S(2)}, u32[]{:S(2)}) collective-permute-start(bf16[2,192,768]{2,1,0:T(8,128)(2,1)S(1)} %copy-done.7), channel_id=1, source_target_pairs={{0,16},{8,24},{16,0},{24,8},{1,17},{9,25},{17,1},{25,9},{2,18},{10... | collective-permute-start | bytes 1769480 | tf_op jit(solution)/shard_map/ppermute | solution.py:167
  149.3 53.2 %collective-permute-start.12 = (bf16[2,192,768]{2,1,0:T(8,128)(2,1)S(1)}, bf16[2,192,768]{2,1,0:T(8,128)(2,1)}, u32[]{:S(2)}, u32[]{:S(2)}) collective-permute-start(bf16[2,192,768]{2,1,0:T(8,128)(2,1)S(1)} %copy-done.6), channel_id=1, source_target_pairs={{0,16},{8,24},{16,0},{24,8},{1,17},{9,25},{17,1},{25,9},{2,18},{10... | collective-permute-start | bytes 1769480 | tf_op jit(solution)/shard_map/ppermute | solution.py:167
  151.7 10.1 %collective-permute-start.5 = (bf16[4,192,192]{2,1,0:T(8,128)(2,1)S(1)}, bf16[4,192,192]{2,1,0:T(8,128)(2,1)S(1)}, u32[]{:S(2)}, u32[]{:S(2)}) collective-permute-start(bf16[4,192,192]{2,1,0:T(8,128)(2,1)S(1)} %get-tuple-element.65), channel_id=1, source_target_pairs={{0,8},{8,0},{16,24},{24,16},{1,9},{9,1},{17,25},{25,17},{2,10},{10... | collective-permute-start | bytes 884744 | tf_op jit(solution)/shard_map/ppermute | solution.py:167
  160.0 33.4 %copy-start.21 = (bf16[4,192,192]{2,1,0:T(8,128)(2,1)}, bf16[4,192,192]{2,1,0:T(8,128)(2,1)S(1)}, u32[]{:S(2)}) copy-start(bf16[4,192,192]{2,1,0:T(8,128)(2,1)S(1)} %collective-permute-done.3.refs_3_) | copy-start | bytes 884740
  160.1 32.8 %collective-permute-start.6 = (bf16[4,192,192]{2,1,0:T(8,128)(2,1)}, bf16[4,192,192]{2,1,0:T(8,128)(2,1)S(1)}, u32[]{:S(2)}, u32[]{:S(2)}) collective-permute-start(bf16[4,192,192]{2,1,0:T(8,128)(2,1)} %get-tuple-element.68), channel_id=1, source_target_pairs={{0,24},{8,16},{16,8},{24,0},{1,25},{9,17},{17,9},{25,1},{2,26},{10... | collective-permute-start | bytes 884744 | tf_op jit(solution)/shard_map/ppermute | solution.py:167
  160.1 33.4 %copy-start.22 = (bf16[4,192,192]{2,1,0:T(8,128)(2,1)}, bf16[4,192,192]{2,1,0:T(8,128)(2,1)S(1)}, u32[]{:S(2)}) copy-start(bf16[4,192,192]{2,1,0:T(8,128)(2,1)S(1)} %collective-permute-done.4.refs_4_) | copy-start | bytes 884740
  160.1 41.1 %collective-permute-start.7 = (bf16[4,192,192]{2,1,0:T(8,128)(2,1)S(1)}, bf16[4,192,192]{2,1,0:T(8,128)(2,1)S(1)}, u32[]{:S(2)}, u32[]{:S(2)}) collective-permute-start(bf16[4,192,192]{2,1,0:T(8,128)(2,1)S(1)} %get-tuple-element.64), channel_id=1, source_target_pairs={{0,24},{8,16},{16,8},{24,0},{1,25},{9,17},{17,9},{25,1},{2,26},{10... | collective-permute-start | bytes 884744 | tf_op jit(solution)/shard_map/ppermute | solution.py:167
  161.8 40.6 %copy-start.23 = (bf16[4,192,192]{2,1,0:T(8,128)(2,1)}, bf16[4,192,192]{2,1,0:T(8,128)(2,1)S(1)}, u32[]{:S(2)}) copy-start(bf16[4,192,192]{2,1,0:T(8,128)(2,1)S(1)} %collective-permute-done.5.refs_5_) | copy-start | bytes 884740
  161.8 53.1 %collective-permute-start.13 = (bf16[2,192,768]{2,1,0:T(8,128)(2,1)S(1)}, bf16[2,192,768]{2,1,0:T(8,128)(2,1)}, u32[]{:S(2)}, u32[]{:S(2)}) collective-permute-start(bf16[2,192,768]{2,1,0:T(8,128)(2,1)S(1)} %copy-done.5), channel_id=1, source_target_pairs={{0,16},{8,24},{16,0},{24,8},{1,17},{9,25},{17,1},{25,9},{2,18},{10... | collective-permute-start | bytes 1769480 | tf_op jit(solution)/shard_map/ppermute | solution.py:167
  192.8 9.6 %copy-start.24 = (bf16[4,192,192]{2,1,0:T(8,128)(2,1)}, bf16[4,192,192]{2,1,0:T(8,128)(2,1)S(1)}, u32[]{:S(2)}) copy-start(bf16[4,192,192]{2,1,0:T(8,128)(2,1)S(1)} %collective-permute-done.6.refs_6_) | copy-start | bytes 884740
  192.8 33.8 %collective-permute-start.14 = (bf16[2,192,768]{2,1,0:T(8,128)(2,1)S(1)}, bf16[2,192,768]{2,1,0:T(8,128)(2,1)}, u32[]{:S(2)}, u32[]{:S(2)}) collective-permute-start(bf16[2,192,768]{2,1,0:T(8,128)(2,1)S(1)} %copy-done.4), channel_id=1, source_target_pairs={{0,16},{8,24},{16,0},{24,8},{1,17},{9,25},{17,1},{25,9},{2,18},{10... | collective-permute-start | bytes 1769480 | tf_op jit(solution)/shard_map/ppermute | solution.py:167
  201.2 25.4 %collective-permute-start.15 = (bf16[2,192,768]{2,1,0:T(8,128)(2,1)S(1)}, bf16[2,192,768]{2,1,0:T(8,128)(2,1)S(1)}, u32[]{:S(2)}, u32[]{:S(2)}) collective-permute-start(bf16[2,192,768]{2,1,0:T(8,128)(2,1)S(1)} %copy-done.7), channel_id=1, source_target_pairs={{0,8},{8,0},{16,24},{24,16},{1,9},{9,1},{17,25},{25,17},{2,10},{10... | collective-permute-start | bytes 1769480 | tf_op jit(solution)/shard_map/ppermute | solution.py:167
  202.4 24.7 %collective-permute-start.16 = (bf16[2,192,768]{2,1,0:T(8,128)(2,1)S(1)}, bf16[2,192,768]{2,1,0:T(8,128)(2,1)S(1)}, u32[]{:S(2)}, u32[]{:S(2)}) collective-permute-start(bf16[2,192,768]{2,1,0:T(8,128)(2,1)S(1)} %copy-done.6), channel_id=1, source_target_pairs={{0,8},{8,0},{16,24},{24,16},{1,9},{9,1},{17,25},{25,17},{2,10},{10... | collective-permute-start | bytes 1769480 | tf_op jit(solution)/shard_map/ppermute | solution.py:167
  202.5 24.7 %collective-permute-start.17 = (bf16[2,192,768]{2,1,0:T(8,128)(2,1)S(1)}, bf16[2,192,768]{2,1,0:T(8,128)(2,1)S(1)}, u32[]{:S(2)}, u32[]{:S(2)}) collective-permute-start(bf16[2,192,768]{2,1,0:T(8,128)(2,1)S(1)} %copy-done.5), channel_id=1, source_target_pairs={{0,8},{8,0},{16,24},{24,16},{1,9},{9,1},{17,25},{25,17},{2,10},{10... | collective-permute-start | bytes 1769480 | tf_op jit(solution)/shard_map/ppermute | solution.py:167
  214.9 17.5 %collective-permute-start.18 = (bf16[2,192,768]{2,1,0:T(8,128)(2,1)S(1)}, bf16[2,192,768]{2,1,0:T(8,128)(2,1)}, u32[]{:S(2)}, u32[]{:S(2)}) collective-permute-start(bf16[2,192,768]{2,1,0:T(8,128)(2,1)S(1)} %copy-done.4), channel_id=1, source_target_pairs={{0,8},{8,0},{16,24},{24,16},{1,9},{9,1},{17,25},{25,17},{2,10},{10... | collective-permute-start | bytes 1769480 | tf_op jit(solution)/shard_map/ppermute | solution.py:167
  226.6 7.2 %collective-permute-start.19 = (bf16[2,192,768]{2,1,0:T(8,128)(2,1)}, bf16[2,192,768]{2,1,0:T(8,128)(2,1)}, u32[]{:S(2)}, u32[]{:S(2)}) collective-permute-start(bf16[2,192,768]{2,1,0:T(8,128)(2,1)} %collective-permute-done.11.refs_16_), channel_id=1, source_target_pairs={{0,8},{8,0},{16,24},{24,16},{1,9},{9,1},{17,25},{25,17},{2,10},{10... | collective-permute-start | bytes 1769480 | tf_op jit(solution)/shard_map/ppermute | solution.py:167
  226.6 7.2 %collective-permute-start.20 = (bf16[2,192,768]{2,1,0:T(8,128)(2,1)}, bf16[2,192,768]{2,1,0:T(8,128)(2,1)S(1)}, u32[]{:S(2)}, u32[]{:S(2)}) collective-permute-start(bf16[2,192,768]{2,1,0:T(8,128)(2,1)} %collective-permute-done.12.refs_17_), channel_id=1, source_target_pairs={{0,8},{8,0},{16,24},{24,16},{1,9},{9,1},{17,25},{25,17},{2,10},{10... | collective-permute-start | bytes 1769480 | tf_op jit(solution)/shard_map/ppermute | solution.py:167
  227.1 6.7 %collective-permute-start.21 = (bf16[2,192,768]{2,1,0:T(8,128)(2,1)}, bf16[2,192,768]{2,1,0:T(8,128)(2,1)S(1)}, u32[]{:S(2)}, u32[]{:S(2)}) collective-permute-start(bf16[2,192,768]{2,1,0:T(8,128)(2,1)} %collective-permute-done.13.refs_18_), channel_id=1, source_target_pairs={{0,8},{8,0},{16,24},{24,16},{1,9},{9,1},{17,25},{25,17},{2,10},{10... | collective-permute-start | bytes 1769480 | tf_op jit(solution)/shard_map/ppermute | solution.py:167
  227.2 6.7 %collective-permute-start.22 = (bf16[2,192,768]{2,1,0:T(8,128)(2,1)}, bf16[2,192,768]{2,1,0:T(8,128)(2,1)S(1)}, u32[]{:S(2)}, u32[]{:S(2)}) collective-permute-start(bf16[2,192,768]{2,1,0:T(8,128)(2,1)} %collective-permute-done.14.refs_19_), channel_id=1, source_target_pairs={{0,8},{8,0},{16,24},{24,16},{1,9},{9,1},{17,25},{25,17},{2,10},{10... | collective-permute-start | bytes 1769480 | tf_op jit(solution)/shard_map/ppermute | solution.py:167
  232.4 14.4 %collective-permute-start.1 = (bf16[48,512]{1,0:T(8,128)(2,1)}, bf16[48,512]{1,0:T(8,128)(2,1)S(1)}, u32[]{:S(2)}, u32[]{:S(2)}) collective-permute-start(bf16[48,512]{1,0:T(8,128)(2,1)} %reduce-scatter.8.cloned.1.call-done), channel_id=1, source_target_pairs={{0,4},{4,0},{1,5},{5,1},{2,6},{6,2},{3,7},{7,3},{8,12},{12,8},{9,1... | collective-permute-start | bytes 147464 | tf_op jit(solution)/shard_map/ppermute | solution.py:167
  235.1 11.7 %copy-start.30 = (bf16[48,512]{1,0:T(8,128)(2,1)S(1)}, bf16[48,512]{1,0:T(8,128)(2,1)}, u32[]{:S(2)}) copy-start(bf16[48,512]{1,0:T(8,128)(2,1)} %reduce-scatter.8.cloned.1.call-done) | copy-start | bytes 147460
  246.8 5.7 %copy-start.1 = (bf16[96,6144]{1,0:T(8,128)(2,1)S(1)}, bf16[96,6144]{1,0:T(8,128)(2,1)}, u32[]{:S(2)}) copy-start(bf16[96,6144]{1,0:T(8,128)(2,1)} %param.8) | copy-start | bytes 3538948
  (16 other events, 29.6 us)
Sparse Core Ops, SparseCore 0:
  44.7 34.8 all-gather.4
  81.2 29.4 all-gather.2
  125.1 18.8 reduce-scatter.7
  146.2 27.4 reduce-scatter.5
  175.9 27.9 reduce-scatter.3

commit v2 on v1

--- a/solution.py
+++ b/solution.py
@@ -6,6 +6,7 @@
 from jax.experimental import pallas as pl
 from jax.experimental.pallas import tpu as pltpu
 from jax.sharding import PartitionSpec as P
+
 
 F32 = jnp.float32
 BF16 = jnp.bfloat16
@@ -42,7 +43,7 @@
 
 def block_chunk(rows, row_base, weight, low, low_out, cot, tok_weight, base, count):
     tokens = rows.shape[0]
-    n_blocks, width_in, width_out = weight.shape
+    _, width_in, width_out = weight.shape
     rank = low.shape[1]
     return pl.pallas_call(
         block_kernel,
@@ -75,27 +76,34 @@
     )(rows, weight, low, low_out, cot, tok_weight)
 
 
-def split_kernel(n_parts, rows, out):
-    part = out.shape[3]
-    value = rows[...]
-    for e in range(n_parts):
-        out[e, 0] = value[:, e * part : (e + 1) * part]
-
-
-def split_rows(rows, n_blocks, n_parts):
+def split_kernel(n_parts, offsets, me, rows, *outs):
+    part = outs[0].shape[2]
+    for out, k in zip(outs, offsets):
+        for e in range(n_parts):
+
+            @pl.when((me[0] ^ k) == e)
+            def _(out=out, e=e):
+                out[0] = rows[:, e * part : (e + 1) * part]
+
+
+def split_rows(me, rows, n_blocks, offsets):
     tokens, width = rows.shape
+    n_parts = len(offsets)
     block_in = width // n_blocks
     part = block_in // n_parts
     return pl.pallas_call(
-        functools.partial(split_kernel, n_parts),
-        grid=(n_blocks,),
-        in_specs=[pl.BlockSpec((tokens, block_in), lambda b: (0, b))],
-        out_specs=pl.BlockSpec((n_parts, 1, tokens, part), lambda b: (0, b, 0, 0)),
-        out_shape=jax.ShapeDtypeStruct((n_parts, n_blocks, tokens, part), BF16),
+        functools.partial(split_kernel, n_parts, offsets),
+        grid_spec=pltpu.PrefetchScalarGridSpec(
+            num_scalar_prefetch=1,
+            grid=(n_blocks,),
+            in_specs=[pl.BlockSpec((tokens, block_in), lambda b, me: (0, b))],
+            out_specs=[pl.BlockSpec((1, tokens, part), lambda b, me: (b, 0, 0))] * n_parts,
+        ),
+        out_shape=[jax.ShapeDtypeStruct((n_blocks, tokens, part), BF16)] * n_parts,
         cost_estimate=pl.CostEstimate(
             flops=0, bytes_accessed=4 * tokens * width, transcendentals=0
         ),
-    )(rows)
+    )(me, rows)
 
 
 def weight_kernel(n_groups, halves, chunks, *refs):
@@ -177,8 +185,26 @@
 def gather_groups(value, masks):
     held = [value]
     for mask in masks:
-        held = held + [swap(x, "dp", mask) for x in held]
+        arrived = []
+        for x in held:
+            arrived.append(swap(x, "dp", mask))
+        held = held + arrived
     return held
+
+
+def col_total(part, direct):
+    if not direct:
+        return lax.psum_scatter(part, "col", scatter_dimension=0, tiled=True).astype(F32)
+    n_col = lax.axis_size("col")
+    me = lax.axis_index("col")
+    shards = part.reshape(n_col, part.shape[0] // n_col, part.shape[1])
+    total = None
+    for k in range(n_col):
+        mine = lax.dynamic_index_in_dim(shards, me ^ k, 0, keepdims=False)
+        if k:
+            mine = swap(mine, "col", k)
+        total = mine.astype(F32) if k == 0 else total + mine.astype(F32)
+    return total
 
 
 def local(
@@ -187,7 +213,7 @@
     n_data = lax.axis_size("dp")
     n_col = lax.axis_size("col")
     my_data = lax.axis_index("dp")
-    n_blocks, block_in, block_out = block_weight.shape
+    n_blocks, block_in, _ = block_weight.shape
     rank_width = lowrank_in.shape[2]
     group_rows = cotangent.shape[0]
     own_rows = group_rows // n_col
@@ -204,7 +230,7 @@
     flat_index = sender * capacity + offset
     my_rows = jnp.take(incoming.reshape(n_data * capacity, incoming.shape[2]), flat_index, axis=0)
 
-    segment_row, _ = lax.optimization_barrier((segments[0], outgoing))
+    segment_row, _ = lax.optimization_barrier((segments[0], my_rows))
     my_alive = jnp.sum(lax.dynamic_index_in_dim(count_table, my_data, 0, keepdims=False))
     weights = doc_weights(segment_row, my_alive)
     out_weights = jnp.take(weights, slot_table, axis=0)
@@ -246,45 +272,43 @@
     chunks = min(4, n_blocks)
     per_chunk = n_blocks // chunks
     acts, grads, in_terms, low_terms, row_parts = [], [], [], [], []
+    me_array = jnp.full((1,), my_data, jnp.int32)
+    direct = n_col <= 4
+    group_slices = [[] for _ in offsets]
     for h in range(halves):
-        row_parts.append(split_rows(panels[h], per_half, n_data))
-    for c in range(chunks):
-        h = c * per_chunk // per_half
-        act, grad, in_term, low_term = block_chunk(
-            panels[h],
-            c * per_chunk - h * per_half,
-            block_weight,
-            panel_low,
-            low_out_blocks,
-            cot_blocks,
-            tok_weight,
-            c * per_chunk,
-            per_chunk,
-        )
-        acts.append(act)
-        grads.append(gather_groups(grad, masks))
-        in_terms.append(in_term)
-        low_terms.append(low_term)
-
-    group_slices, group_lows = [], []
+        row_parts.append(split_rows(me_array, panels[h], per_half, offsets))
+        for at, k in enumerate(offsets):
+            piece = row_parts[h][at]
+            group_slices[at].append(swap(piece, "dp", k) if k else piece)
+        for c in range(h * chunks // halves, (h + 1) * chunks // halves):
+            act, grad, in_term, low_term = block_chunk(
+                panels[h],
+                c * per_chunk - h * per_half,
+                block_weight,
+                panel_low,
+                low_out_blocks,
+                cot_blocks,
+                tok_weight,
+                c * per_chunk,
+                per_chunk,
+            )
+            acts.append(act)
+            grads.append(gather_groups(grad, masks))
+            in_terms.append(in_term)
+            low_terms.append(low_term)
+
+    group_lows = []
     for k in offsets:
-        pieces = []
-        for h in range(halves):
-            piece = lax.dynamic_index_in_dim(row_parts[h], my_data ^ k, 0, keepdims=False)
-            pieces.append(swap(piece, "dp", k) if k else piece)
-        group_slices.append(pieces)
         low_piece = lax.dynamic_index_in_dim(low_split, my_data ^ k, 0, keepdims=False)
         group_lows.append(swap(low_piece, "dp", k) if k else low_piece)
 
-    own_low_term = lax.psum_scatter(
-        sum(low_terms).astype(BF16), "col", scatter_dimension=0, tiled=True
-    )
+    own_low_term = col_total(sum(low_terms).astype(BF16), direct)
     low_grad = row_total(own_low_term).astype(BF16)
     half_chunks = chunks // halves
     terms = []
     for h in range(halves):
         part = jnp.concatenate(in_terms[h * half_chunks : (h + 1) * half_chunks], axis=1)
-        terms.append(lax.psum_scatter(part, "col", scatter_dimension=0, tiled=True))
+        terms.append(col_total(part, direct))
     own_term = jnp.concatenate(terms, axis=1).astype(F32)
     input_grad = (own_term + dot(low_grad, flat_in, 1, 1)).astype(BF16)
 
@@ -311,4 +335,5 @@
         P("dp", "row", "col"),
         P("dp", "row", "col"),
     )
+
     return jax.shard_map(local, mesh=mesh, in_specs=in_specs, out_specs=out_specs, check_vma=False)

time: 260 us -> 277 us (1.065)
  starting transfers between devices: 24.7 us -> 44.9 us
  other arithmetic: 15.8 us -> 18.9 us
  matrix products: 9.67 us -> 6.74 us
    ppermute x23 -> x32, starting transfers between devices: 16.5 us -> 37.3 us  [swap(): lax.ppermute(value, axis, [(s, s ^ mask) for s in range(lax.axis_size(axi...]
    ppermute x23 -> x32, waiting for transfers between devices: 70.9 us -> 87 us  [swap(): lax.ppermute(value, axis, [(s, s ^ mask) for s in range(lax.axis_size(axi...]
    all_gather x2, waiting for transfers between devices: 20.5 us -> 7.47 us  [local(): panels.append(lax.all_gather(piece, 'col', axis=0, tiled=True))]
    all_to_all x1, waiting for transfers between devices: 3.34 us -> 0.01 us  [local(): lax.all_to_all(out_weights, 'dp', split_axis=0, concat_axis=0, tiled=True)]
    squeeze x2 -> x3, local copies, waits for them, and re-layouts: 4.95 us -> 1.88 us  [col_total(): mine = lax.dynamic_index_in_dim(shards, me ^ k, 0, keepdims=False)]
    dot_general x1, matrix products: 5.71 us -> 2.75 us  [dot(): lax.dot_general(left, right, (((left_dim,), (right_dim,)), ((), ())), pre...]
    unnamed x75 -> x101, local copies, waits for them, and re-layouts: 15.6 us -> 16.8 us
  transfers between devices with their start and end apart: 30 -> 36, of which waited for: 10 -> 11; matrix products, arithmetic and copies ran while one was open for 14% -> 15% of each run, Pallas kernels for 12% -> 12%
where the time goes in v2:
time: 277 us; the launch traced here: 276 us
  waiting for transfers between devices  104 us (38%)
  starting transfers between devices  44.9 us (16%)
  Pallas kernels  44.5 us (16%)
  local copies, waits for them, and re-layouts  27.3 us (10%)
  other arithmetic  18.9 us (7%)
  blocking collectives  15.2 us (5%)
  between operations  14.7 us (5%)
  matrix products  6.74 us (2%)
    ppermute x32, waiting for transfers between devices, swap(): lax.ppermute(value, axis, [(s, s ^ mask) for s in range(lax.axis_size(axi...  87 us
    ppermute x32, starting transfers between devices, swap(): lax.ppermute(value, axis, [(s, s ^ mask) for s in range(lax.axis_size(axi...  37.3 us
    pallas_call x4, Pallas kernels, block_chunk(): pl.pallas_call(block_kernel, grid=(count,), in_specs=[pl.BlockSpec((token...  24.7 us
    unnamed x101, local copies, waits for them, and re-layouts  16.8 us
    all_gather x1, blocking collectives, local(): extra = lax.all_gather(own_extra, 'col', axis=0, tiled=True)  15.2 us
    pallas_call x1, Pallas kernels, weight_grads(): pl.pallas_call(functools.partial(weight_kernel, n_groups, halves, chunks)...  11.7 us
    all_to_all x1, waiting for transfers between devices, local(): lax.all_to_all(outgoing, 'dp', split_axis=0, concat_axis=0, tiled=True)  9.37 us
    pallas_call x2, Pallas kernels, split_rows(): pl.pallas_call(functools.partial(split_kernel, n_parts, offsets), grid_sp...  8.04 us
  transfers between devices with their start and end apart: 36, of which 11 were waited for; matrix products, arithmetic and copies ran while one was open for 15% of the time, Pallas kernels for 12%

profile of v2, /device:TPU:0, one launch (start us, length us, event | category | flops | bytes accessed | tf_op | source)
XLA Modules:
  0.0 276.1 jit_solution(5667860095767863494)
XLA Ops:
  8.7 1.2 gather_fusion
  11.5 4.4 %all-to-all-start = ((bf16[4,23,6144]{2,1,0:T(8,128)(2,1)}), bf16[4,23,6144]{2,1,0:T(8,128)(2,1)S(1)}, u32[]{:S(2)}, u32[]{:S(2)}) async-start(bf16[4,23,6144]{2,1,0:T(8,128)(2,1)} %broadcast_select_fusion), calls=%async_computation | async-start | bytes 2359296 | tf_op jit(solution)/shard_map/all_to_all | solution.py:223
  17.1 2.7 fusion.12
  19.7 2.7 compare_and_fusion.1
  22.4 9.4 %all-to-all-done = bf16[4,23,6144]{2,1,0:T(8,128)(2,1)S(1)} async-done(((bf16[4,23,6144]{2,1,0:T(8,128)(2,1)}), bf16[4,23,6144]{2,1,0:T(8,128)(2,1)S(1)}, u32[]{:S(2)}, u32[]{:S(2)}) %all-to-all-start) | async-done | bytes 1130528 | tf_op jit(solution)/shard_map/all_to_all | solution.py:223
  34.7 6.8 %copy.60 = bf16[512,8,768]{2,0,1:T(8,128)(2,1)} copy(bf16[512,8,768]{2,1,0:T(8,128)(2,1)} %param.14) | data formatting | bytes 12582912 | tf_op args[6]
  41.5 1.9 copy.61
  44.3 1.2 gather_fusion.2
  46.2 3.2 %all-to-all-start.1 = ((bf16[4,1,23]{2,1,0:T(2,128)(2,1)}), bf16[4,1,23]{2,1,0:T(2,128)(2,1)S(1)}, u32[]{:S(2)}, u32[]{:S(2)}) async-start(bf16[4,1,23]{2,1,0:T(2,128)(2,1)} %copy.42), calls=%async_computation.1 | async-start | bytes 4096 | tf_op jit(solution)/shard_map/all_to_all | solution.py:237
  49.5 4.0 %convolution_convert_fusion = bf16[48,512]{1,0:T(8,128)(2,1)S(1)} fusion(bf16[48,6144]{1,0:T(8,128)(2,1)S(1)} %broadcast_select_fusion.1, bf16[6144,512]{1,0:T(8,128)(2,1)} %bitcast.120), kind=kOutput, calls=%fused_computation.12 | convolution fusion | flops 302014464 | bytes 6930432 | tf_op jit(solution)/shard_map/dot_general | solution.py:241
  53.5 2.3 collective-permute-start
  56.6 2.7 broadcast_select_fusion.2
  59.4 15.2 %all_gather.10 = bf16[192,640]{1,0:T(8,128)(2,1)S(1)} all-gather(bf16[48,640]{1,0:T(8,128)(2,1)S(1)} %pad_maximum_fusion.2), channel_id=1, replica_groups=mesh['dp'=4,'row'=2,'col'=4] {'col'}, dimensions={0}, use_global_device_ids=true | all-gather | bytes 307200 | tf_op jit(solution)/shard_map/all_gather | solution.py:254
  75.7 1.5 collective-permute-start.17
  78.0 6.3 %shard_map.114 = (bf16[2,192,768]{2,1,0:T(8,128)(2,1)}, bf16[2,192,768]{2,1,0:T(8,128)(2,1)}, bf16[192,1536]{1,0:T(8,128)(2,1)}, f32[192,512]{1,0:T(8,128)}) custom-call(bf16[192,3072]{1,0:T(8,128)(2,1)} %all-gather.5.cloned.1.call-done.rows, bf16[8,768,768]{2,1,0:T(8,128)(2,1)} %weight.7, bf16[192,512]{1,0:T(8,128)(2,1)} %copy-done.2, ...), custom_call_target="tpu_custom_call" | custom-call | flops 1509949440 | bytes 5701632 | tf_op jit(solution)/shard_map/pallas_call | solution.py:48
  84.3 6.1 %shard_map.113 = (bf16[2,192,768]{2,1,0:T(8,128)(2,1)}, bf16[2,192,768]{2,1,0:T(8,128)(2,1)}, bf16[192,1536]{1,0:T(8,128)(2,1)}, f32[192,512]{1,0:T(8,128)}) custom-call(bf16[192,3072]{1,0:T(8,128)(2,1)} %all-gather.5.cloned.1.call-done.rows, bf16[8,768,768]{2,1,0:T(8,128)(2,1)} %weight.7, bf16[192,512]{1,0:T(8,128)(2,1)} %copy-done.2, ...), custom_call_target="tpu_custom_call" | custom-call | flops 1509949440 | bytes 5701632 | tf_op jit(solution)/shard_map/pallas_call | solution.py:48
  90.4 7.5 %all-gather.3.cloned.1.call-done.rows = bf16[192,3072]{1,0:T(8,128)(2,1)} async-done(((bf16[48,3072]{1,0:T(8,128)(2,1)}), bf16[192,3072]{1,0:T(8,128)(2,1)}) %all-gather.3.cloned.1.call-update) | async-done | bytes 1179664 | tf_op jit(solution)/shard_map/all_gather | solution.py:252
  97.9 6.2 %shard_map.112 = (bf16[2,192,768]{2,1,0:T(8,128)(2,1)}, bf16[2,192,768]{2,1,0:T(8,128)(2,1)}, bf16[192,1536]{1,0:T(8,128)(2,1)}, f32[192,512]{1,0:T(8,128)}) custom-call(bf16[192,3072]{1,0:T(8,128)(2,1)} %all-gather.3.cloned.1.call-done.rows, bf16[8,768,768]{2,1,0:T(8,128)(2,1)} %weight.7, bf16[192,512]{1,0:T(8,128)(2,1)} %copy-done.2, ...), custom_call_target="tpu_custom_call" | custom-call | flops 1509949440 | bytes 5701632 | tf_op jit(solution)/shard_map/pallas_call | solution.py:48
  104.1 6.2 %shard_map.111 = (bf16[2,192,768]{2,1,0:T(8,128)(2,1)}, bf16[2,192,768]{2,1,0:T(8,128)(2,1)}, bf16[192,1536]{1,0:T(8,128)(2,1)}, f32[192,512]{1,0:T(8,128)}) custom-call(bf16[192,3072]{1,0:T(8,128)(2,1)} %all-gather.3.cloned.1.call-done.rows, bf16[8,768,768]{2,1,0:T(8,128)(2,1)} %weight.7, bf16[192,512]{1,0:T(8,128)(2,1)} %copy-done.2, ...), custom_call_target="tpu_custom_call" | custom-call | flops 1509949440 | bytes 5701632 | tf_op jit(solution)/shard_map/pallas_call | solution.py:48
  110.4 1.2 add_convert_fusion
  111.6 1.7 collective-permute-start.9
  114.3 1.7 collective-permute-start.7
  119.1 2.0 collective-permute-start.6
  121.2 1.7 collective-permute-start.10
  123.9 2.1 collective-permute-start.4
  126.0 2.2 collective-permute-start.3
  128.3 2.7 collective-permute-done.6
  130.9 10.6 %collective-permute-start.1 = (bf16[48,3072]{1,0:T(8,128)(2,1)}, bf16[48,3072]{1,0:T(8,128)(2,1)}, u32[]{:S(2)}, u32[]{:S(2)}) collective-permute-start(bf16[48,3072]{1,0:T(8,128)(2,1)} %get-tuple-element.78), channel_id=1, source_target_pairs={{0,1},{1,0},{2,3},{3,2},{4,5},{5,4},{6,7},{7,6},{8,9},{9,8},{10,11... | collective-permute-start | bytes 884744 | tf_op jit(solution)/shard_map/ppermute | solution.py:175
  141.6 4.0 %shard_map.115 = (bf16[4,192,192]{2,1,0:T(8,128)(2,1)}, bf16[4,192,192]{2,1,0:T(8,128)(2,1)}, bf16[4,192,192]{2,1,0:T(8,128)(2,1)}, bf16[4,192,192]{2,1,0:T(8,128)(2,1)}) custom-call(s32[1]{0:T(128)} %bitcast.32.me, bf16[192,3072]{1,0:T(8,128)(2,1)} %all-gather.3.cloned.1.call-done.rows), custom_call_target="tpu_custom_call" | custom-call | bytes 2359296 | tf_op jit(solution)/shard_map/pallas_call | solution.py:94
  145.6 4.0 %shard_map.116 = (bf16[4,192,192]{2,1,0:T(8,128)(2,1)}, bf16[4,192,192]{2,1,0:T(8,128)(2,1)}, bf16[4,192,192]{2,1,0:T(8,128)(2,1)}, bf16[4,192,192]{2,1,0:T(8,128)(2,1)}) custom-call(s32[1]{0:T(128)} %bitcast.32.me, bf16[192,3072]{1,0:T(8,128)(2,1)} %all-gather.5.cloned.1.call-done.rows), custom_call_target="tpu_custom_call" | custom-call | bytes 2359296 | tf_op jit(solution)/shard_map/pallas_call | solution.py:94
  149.6 10.4 %collective-permute-done.5 = bf16[48,3072]{1,0:T(8,128)(2,1)} collective-permute-done((bf16[48,3072]{1,0:T(8,128)(2,1)}, bf16[48,3072]{1,0:T(8,128)(2,1)}, u32[]{:S(2)}, u32[]{:S(2)}) %collective-permute-start.5) | collective-permute-done | bytes 294944 | tf_op jit(solution)/shard_map/ppermute | solution.py:175
  160.1 1.7 collective-permute-start.11
  162.1 10.6 %collective-permute-done.2 = bf16[48,3072]{1,0:T(8,128)(2,1)} collective-permute-done((bf16[48,3072]{1,0:T(8,128)(2,1)}, bf16[48,3072]{1,0:T(8,128)(2,1)}, u32[]{:S(2)}, u32[]{:S(2)}) %collective-permute-start.2) | collective-permute-done | bytes 294944 | tf_op jit(solution)/shard_map/ppermute | solution.py:175
  173.5 1.2 collective-permute-start.21
  174.8 5.9 %collective-permute-done.12.refs_3_ = bf16[4,192,192]{2,1,0:T(8,128)(2,1)S(1)} collective-permute-done((bf16[4,192,192]{2,1,0:T(8,128)(2,1)}, bf16[4,192,192]{2,1,0:T(8,128)(2,1)S(1)}, u32[]{:S(2)}, u32[]{:S(2)}) %collective-permute-start.12) | collective-permute-done | bytes 294944 | tf_op jit(solution)/shard_map/ppermute | solution.py:175
  180.7 1.7 collective-permute-start.16
  182.5 1.5 copy.65
  184.0 1.7 maximum_bitcast_fusion
  185.7 2.7 copy.49
  188.7 25.1 %collective-permute-done.15.refs_6_ = bf16[4,192,192]{2,1,0:T(8,128)(2,1)S(1)} collective-permute-done((bf16[4,192,192]{2,1,0:T(8,128)(2,1)}, bf16[4,192,192]{2,1,0:T(8,128)(2,1)S(1)}, u32[]{:S(2)}, u32[]{:S(2)}) %collective-permute-start.15) | collective-permute-done | bytes 294944 | tf_op jit(solution)/shard_map/ppermute | solution.py:175
  214.5 6.7 %collective-permute-done.16.refs_7_ = bf16[4,192,192]{2,1,0:T(8,128)(2,1)S(1)} collective-permute-done((bf16[4,192,192]{2,1,0:T(8,128)(2,1)}, bf16[4,192,192]{2,1,0:T(8,128)(2,1)S(1)}, u32[]{:S(2)}, u32[]{:S(2)}) %collective-permute-start.16) | collective-permute-done | bytes 294944 | tf_op jit(solution)/shard_map/ppermute | solution.py:175
  221.9 1.7 collective-permute-start.23
  223.7 1.2 fusion.2
  224.9 12.5 %collective-permute-done.22.refs_18_ = bf16[2,192,768]{2,1,0:T(8,128)(2,1)S(1)} collective-permute-done((bf16[2,192,768]{2,1,0:T(8,128)(2,1)S(1)}, bf16[2,192,768]{2,1,0:T(8,128)(2,1)S(1)}, u32[]{:S(2)}, u32[]{:S(2)}) %collective-permute-start.22) | collective-permute-done | bytes 589856 | tf_op jit(solution)/shard_map/ppermute | solution.py:175
  237.4 12.3 %collective-permute-done.23.refs_19_ = bf16[2,192,768]{2,1,0:T(8,128)(2,1)S(1)} collective-permute-done((bf16[2,192,768]{2,1,0:T(8,128)(2,1)S(1)}, bf16[2,192,768]{2,1,0:T(8,128)(2,1)S(1)}, u32[]{:S(2)}, u32[]{:S(2)}) %collective-permute-start.23) | collective-permute-done | bytes 589856 | tf_op jit(solution)/shard_map/ppermute | solution.py:175
  251.6 1.3 fusion.4
  252.9 2.8 fusion
  257.5 11.7 %shard_map.117 = (f32[192,8,768]{2,1,0:T(8,128)}, f32[128,8,768]{2,1,0:T(8,128)}) custom-call(bf16[4,192,192]{2,1,0:T(8,128)(2,1)} %get-tuple-element.44.refs_0_, bf16[4,192,192]{2,1,0:T(8,128)(2,1)} %get-tuple-element.45.refs_1_, bf16[4,192,192]{2,1,0:T(8,128)(2,1)} %copy-done.24, bf16[4,192,192]{2,1,0:T(8,128)(2,1)} %copy-done.25, ...), custom_call_target="tpu_custom_call" | custom-call | flops 3019898880 | bytes 17301504 | tf_op jit(solution)/shard_map/pallas_call | solution.py:143
  (186 shorter events, 23.3 us)
Async XLA Ops:
  11.5 20.2 %all-to-all-start = ((bf16[4,23,6144]{2,1,0:T(8,128)(2,1)}), bf16[4,23,6144]{2,1,0:T(8,128)(2,1)S(1)}, u32[]{:S(2)}, u32[]{:S(2)}) async-start(bf16[4,23,6144]{2,1,0:T(8,128)(2,1)} %broadcast_select_fusion), calls=%async_computation | async-start | bytes 2359296 | tf_op jit(solution)/shard_map/all_to_all | solution.py:223
  15.9 62.1 %all-gather.5.cloned.1.call-start = ((), (), s32[]{:S(2)}) async-start(), calls=%async_computation.3 | async-start | bytes 1474560 | tf_op jit(solution)/shard_map/all_gather | solution.py:252
  34.0 63.8 %all-gather.3.cloned.1.call-start = ((), (), s32[]{:S(2)}) async-start(), calls=%async_computation.2 | async-start | bytes 1474560 | tf_op jit(solution)/shard_map/all_gather | solution.py:252
  46.2 9.5 %all-to-all-start.1 = ((bf16[4,1,23]{2,1,0:T(2,128)(2,1)}), bf16[4,1,23]{2,1,0:T(2,128)(2,1)S(1)}, u32[]{:S(2)}, u32[]{:S(2)}) async-start(bf16[4,1,23]{2,1,0:T(2,128)(2,1)} %copy.42), calls=%async_computation.1 | async-start | bytes 4096 | tf_op jit(solution)/shard_map/all_to_all | solution.py:237
  53.5 5.8 %collective-permute-start = (bf16[48,512]{1,0:T(8,128)(2,1)S(1)}, bf16[48,512]{1,0:T(8,128)(2,1)S(1)}, u32[]{:S(2)}, u32[]{:S(2)}) collective-permute-start(bf16[48,512]{1,0:T(8,128)(2,1)S(1)} %convolution_convert_fusion), channel_id=1, source_target_pairs={{0,4},{4,0},{1,5},{5,1},{2,6},{6,2},{3,7},{7,3},{8,12},{12,8},{9,1... | collective-permute-start | bytes 147464 | tf_op jit(solution)/shard_map/ppermute | solution.py:175
  75.7 48.1 %collective-permute-start.17 = (bf16[192,128]{1,0:T(8,128)(2,1)S(1)}, bf16[192,128]{1,0:T(8,128)(2,1)S(1)}, u32[]{:S(2)}, u32[]{:S(2)}) collective-permute-start(bf16[192,128]{1,0:T(8,128)(2,1)S(1)} %bitcast.133), channel_id=1, source_target_pairs={{0,16},{8,24},{16,0},{24,8},{1,17},{9,25},{17,1},{25,9},{2,18},{10... | collective-permute-start | bytes 147464 | tf_op jit(solution)/shard_map/ppermute | solution.py:175
  77.3 46.6 %collective-permute-start.18 = (bf16[192,128]{1,0:T(8,128)(2,1)S(1)}, bf16[192,128]{1,0:T(8,128)(2,1)S(1)}, u32[]{:S(2)}, u32[]{:S(2)}) collective-permute-start(bf16[192,128]{1,0:T(8,128)(2,1)S(1)} %bitcast.132), channel_id=1, source_target_pairs={{0,8},{8,0},{16,24},{24,16},{1,9},{9,1},{17,25},{25,17},{2,10},{10... | collective-permute-start | bytes 147464 | tf_op jit(solution)/shard_map/ppermute | solution.py:175
  111.6 6.7 %collective-permute-start.9 = (bf16[48,512]{1,0:T(8,128)(2,1)S(1)}, bf16[48,512]{1,0:T(8,128)(2,1)S(1)}, u32[]{:S(2)}, u32[]{:S(2)}) collective-permute-start(bf16[48,512]{1,0:T(8,128)(2,1)S(1)} %get-tuple-element.91), channel_id=1, source_target_pairs={{0,3},{1,2},{2,1},{3,0},{4,7},{5,6},{6,5},{7,4},{8,11},{9,10},{10,... | collective-permute-start | bytes 147464 | tf_op jit(solution)/shard_map/ppermute | solution.py:175
  113.3 5.8 %collective-permute-start.8 = (bf16[48,512]{1,0:T(8,128)(2,1)S(1)}, bf16[48,512]{1,0:T(8,128)(2,1)S(1)}, u32[]{:S(2)}, u32[]{:S(2)}) collective-permute-start(bf16[48,512]{1,0:T(8,128)(2,1)S(1)} %get-tuple-element.92), channel_id=1, source_target_pairs={{0,2},{1,3},{2,0},{3,1},{4,6},{5,7},{6,4},{7,5},{8,10},{9,11},{10,... | collective-permute-start | bytes 147464 | tf_op jit(solution)/shard_map/ppermute | solution.py:175
  114.3 6.8 %collective-permute-start.7 = (bf16[48,512]{1,0:T(8,128)(2,1)S(1)}, bf16[48,512]{1,0:T(8,128)(2,1)S(1)}, u32[]{:S(2)}, u32[]{:S(2)}) collective-permute-start(bf16[48,512]{1,0:T(8,128)(2,1)S(1)} %get-tuple-element.90), channel_id=1, source_target_pairs={{0,1},{1,0},{2,3},{3,2},{4,5},{5,4},{6,7},{7,6},{8,9},{9,8},{10,11... | collective-permute-start | bytes 147464 | tf_op jit(solution)/shard_map/ppermute | solution.py:175
  118.3 7.7 %collective-permute-start.19 = (bf16[192,128]{1,0:T(8,128)(2,1)S(1)}, bf16[192,128]{1,0:T(8,128)(2,1)S(1)}, u32[]{:S(2)}, u32[]{:S(2)}) collective-permute-start(bf16[192,128]{1,0:T(8,128)(2,1)S(1)} %bitcast.131), channel_id=1, source_target_pairs={{0,24},{8,16},{16,8},{24,0},{1,25},{9,17},{17,9},{25,1},{2,26},{10... | collective-permute-start | bytes 147464 | tf_op jit(solution)/shard_map/ppermute | solution.py:175
  119.1 11.8 %collective-permute-start.6 = (bf16[48,3072]{1,0:T(8,128)(2,1)S(1)}, bf16[48,3072]{1,0:T(8,128)(2,1)S(1)}, u32[]{:S(2)}, u32[]{:S(2)}) collective-permute-start(bf16[48,3072]{1,0:T(8,128)(2,1)S(1)} %get-tuple-element.82), channel_id=1, source_target_pairs={{0,3},{1,2},{2,1},{3,0},{4,7},{5,6},{6,5},{7,4},{8,11},{9,10},{10,... | collective-permute-start | bytes 884744 | tf_op jit(solution)/shard_map/ppermute | solution.py:175
  121.2 7.1 %collective-permute-start.10 = (bf16[48,512]{1,0:T(8,128)(2,1)S(1)}, bf16[48,512]{1,0:T(8,128)(2,1)S(1)}, u32[]{:S(2)}, u32[]{:S(2)}) collective-permute-start(bf16[48,512]{1,0:T(8,128)(2,1)S(1)} %fusion.7), channel_id=1, source_target_pairs={{0,4},{4,0},{1,5},{5,1},{2,6},{6,2},{3,7},{7,3},{8,12},{12,8},{9,1... | collective-permute-start | bytes 147464 | tf_op jit(solution)/shard_map/ppermute | solution.py:175
  123.9 36.2 %collective-permute-start.5 = (bf16[48,3072]{1,0:T(8,128)(2,1)}, bf16[48,3072]{1,0:T(8,128)(2,1)}, u32[]{:S(2)}, u32[]{:S(2)}) collective-permute-start(bf16[48,3072]{1,0:T(8,128)(2,1)} %get-tuple-element.83), channel_id=1, source_target_pairs={{0,2},{1,3},{2,0},{3,1},{4,6},{5,7},{6,4},{7,5},{8,10},{9,11},{10,... | collective-permute-start | bytes 884744 | tf_op jit(solution)/shard_map/ppermute | solution.py:175
  123.9 37.9 %collective-permute-start.4 = (bf16[48,3072]{1,0:T(8,128)(2,1)}, bf16[48,3072]{1,0:T(8,128)(2,1)}, u32[]{:S(2)}, u32[]{:S(2)}) collective-permute-start(bf16[48,3072]{1,0:T(8,128)(2,1)} %get-tuple-element.81), channel_id=1, source_target_pairs={{0,1},{1,0},{2,3},{3,2},{4,5},{5,4},{6,7},{7,6},{8,9},{9,8},{10,11... | collective-permute-start | bytes 884744 | tf_op jit(solution)/shard_map/ppermute | solution.py:175
  126.0 36.1 %collective-permute-start.3 = (bf16[48,3072]{1,0:T(8,128)(2,1)}, bf16[48,3072]{1,0:T(8,128)(2,1)}, u32[]{:S(2)}, u32[]{:S(2)}) collective-permute-start(bf16[48,3072]{1,0:T(8,128)(2,1)} %get-tuple-element.79), channel_id=1, source_target_pairs={{0,3},{1,2},{2,1},{3,0},{4,7},{5,6},{6,5},{7,4},{8,11},{9,10},{10,... | collective-permute-start | bytes 884744 | tf_op jit(solution)/shard_map/ppermute | solution.py:175
  128.3 44.5 %collective-permute-start.2 = (bf16[48,3072]{1,0:T(8,128)(2,1)}, bf16[48,3072]{1,0:T(8,128)(2,1)}, u32[]{:S(2)}, u32[]{:S(2)}) collective-permute-start(bf16[48,3072]{1,0:T(8,128)(2,1)} %get-tuple-element.80), channel_id=1, source_target_pairs={{0,2},{1,3},{2,0},{3,1},{4,6},{5,7},{6,4},{7,5},{8,10},{9,11},{10,... | collective-permute-start | bytes 884744 | tf_op jit(solution)/shard_map/ppermute | solution.py:175
  130.9 42.6 %collective-permute-start.1 = (bf16[48,3072]{1,0:T(8,128)(2,1)}, bf16[48,3072]{1,0:T(8,128)(2,1)}, u32[]{:S(2)}, u32[]{:S(2)}) collective-permute-start(bf16[48,3072]{1,0:T(8,128)(2,1)} %get-tuple-element.78), channel_id=1, source_target_pairs={{0,1},{1,0},{2,3},{3,2},{4,5},{5,4},{6,7},{7,6},{8,9},{9,8},{10,11... | collective-permute-start | bytes 884744 | tf_op jit(solution)/shard_map/ppermute | solution.py:175
  141.6 42.4 %copy-start.6 = (bf16[2,192,768]{2,1,0:T(8,128)(2,1)S(1)}, bf16[2,192,768]{2,1,0:T(8,128)(2,1)}, u32[]{:S(2)}) copy-start(bf16[2,192,768]{2,1,0:T(8,128)(2,1)} %get-tuple-element.35) | copy-start | bytes 1769476
  141.6 42.4 %copy-start.7 = (bf16[2,192,768]{2,1,0:T(8,128)(2,1)S(1)}, bf16[2,192,768]{2,1,0:T(8,128)(2,1)}, u32[]{:S(2)}) copy-start(bf16[2,192,768]{2,1,0:T(8,128)(2,1)} %get-tuple-element.34) | copy-start | bytes 1769476
  160.1 14.7 %collective-permute-start.11 = (bf16[4,192,192]{2,1,0:T(8,128)(2,1)}, bf16[4,192,192]{2,1,0:T(8,128)(2,1)S(1)}, u32[]{:S(2)}, u32[]{:S(2)}) collective-permute-start(bf16[4,192,192]{2,1,0:T(8,128)(2,1)} %get-tuple-element.46), channel_id=1, source_target_pairs={{0,16},{8,24},{16,0},{24,8},{1,17},{9,25},{17,1},{25,9},{2,18},{10... | collective-permute-start | bytes 884744 | tf_op jit(solution)/shard_map/ppermute | solution.py:175
  161.8 18.9 %collective-permute-start.12 = (bf16[4,192,192]{2,1,0:T(8,128)(2,1)}, bf16[4,192,192]{2,1,0:T(8,128)(2,1)S(1)}, u32[]{:S(2)}, u32[]{:S(2)}) collective-permute-start(bf16[4,192,192]{2,1,0:T(8,128)(2,1)} %get-tuple-element.47), channel_id=1, source_target_pairs={{0,16},{8,24},{16,0},{24,8},{1,17},{9,25},{17,1},{25,9},{2,18},{10... | collective-permute-start | bytes 884744 | tf_op jit(solution)/shard_map/ppermute | solution.py:175
  162.1 18.6 %collective-permute-start.13 = (bf16[4,192,192]{2,1,0:T(8,128)(2,1)}, bf16[4,192,192]{2,1,0:T(8,128)(2,1)S(1)}, u32[]{:S(2)}, u32[]{:S(2)}) collective-permute-start(bf16[4,192,192]{2,1,0:T(8,128)(2,1)} %get-tuple-element.48), channel_id=1, source_target_pairs={{0,8},{8,0},{16,24},{24,16},{1,9},{9,1},{17,25},{25,17},{2,10},{10... | collective-permute-start | bytes 884744 | tf_op jit(solution)/shard_map/ppermute | solution.py:175
  172.7 49.0 %collective-permute-start.20 = (bf16[2,192,768]{2,1,0:T(8,128)(2,1)}, bf16[2,192,768]{2,1,0:T(8,128)(2,1)S(1)}, u32[]{:S(2)}, u32[]{:S(2)}) collective-permute-start(bf16[2,192,768]{2,1,0:T(8,128)(2,1)} %get-tuple-element.52.refs_12_), channel_id=1, source_target_pairs={{0,16},{8,24},{16,0},{24,8},{1,17},{9,25},{17,1},{25,9},{2,18},{10... | collective-permute-start | bytes 1769480 | tf_op jit(solution)/shard_map/ppermute | solution.py:175
  173.5 48.4 %collective-permute-start.21 = (bf16[2,192,768]{2,1,0:T(8,128)(2,1)}, bf16[2,192,768]{2,1,0:T(8,128)(2,1)S(1)}, u32[]{:S(2)}, u32[]{:S(2)}) collective-permute-start(bf16[2,192,768]{2,1,0:T(8,128)(2,1)} %get-tuple-element.53.refs_13_), channel_id=1, source_target_pairs={{0,16},{8,24},{16,0},{24,8},{1,17},{9,25},{17,1},{25,9},{2,18},{10... | collective-permute-start | bytes 1769480 | tf_op jit(solution)/shard_map/ppermute | solution.py:175
  174.7 13.7 %collective-permute-start.14 = (bf16[4,192,192]{2,1,0:T(8,128)(2,1)}, bf16[4,192,192]{2,1,0:T(8,128)(2,1)S(1)}, u32[]{:S(2)}, u32[]{:S(2)}) collective-permute-start(bf16[4,192,192]{2,1,0:T(8,128)(2,1)} %get-tuple-element.49), channel_id=1, source_target_pairs={{0,8},{8,0},{16,24},{24,16},{1,9},{9,1},{17,25},{25,17},{2,10},{10... | collective-permute-start | bytes 884744 | tf_op jit(solution)/shard_map/ppermute | solution.py:175
  180.7 33.1 %collective-permute-start.15 = (bf16[4,192,192]{2,1,0:T(8,128)(2,1)}, bf16[4,192,192]{2,1,0:T(8,128)(2,1)S(1)}, u32[]{:S(2)}, u32[]{:S(2)}) collective-permute-start(bf16[4,192,192]{2,1,0:T(8,128)(2,1)} %get-tuple-element.50), channel_id=1, source_target_pairs={{0,24},{8,16},{16,8},{24,0},{1,25},{9,17},{17,9},{25,1},{2,26},{10... | collective-permute-start | bytes 884744 | tf_op jit(solution)/shard_map/ppermute | solution.py:175
  180.7 40.5 %collective-permute-start.16 = (bf16[4,192,192]{2,1,0:T(8,128)(2,1)}, bf16[4,192,192]{2,1,0:T(8,128)(2,1)S(1)}, u32[]{:S(2)}, u32[]{:S(2)}) collective-permute-start(bf16[4,192,192]{2,1,0:T(8,128)(2,1)} %get-tuple-element.51), channel_id=1, source_target_pairs={{0,24},{8,16},{16,8},{24,0},{1,25},{9,17},{17,9},{25,1},{2,26},{10... | collective-permute-start | bytes 884744 | tf_op jit(solution)/shard_map/ppermute | solution.py:175
  184.0 68.9 %slice-start = ((s8[6291456]{0:T(1024)(128)(4,1)}), s8[4194304]{0:T(1024)(128)(4,1)S(1)}, s32[]{:S(2)}) async-start(s8[6291456]{0:T(1024)(128)(4,1)} %bitcast.121), calls=%async_computation.4 | async-start | bytes 8388608
  185.7 35.5 %copy-start.5 = (bf16[2,192,768]{2,1,0:T(8,128)(2,1)S(1)}, bf16[2,192,768]{2,1,0:T(8,128)(2,1)}, u32[]{:S(2)}) copy-start(bf16[2,192,768]{2,1,0:T(8,128)(2,1)} %get-tuple-element.54.refs_14_) | copy-start | bytes 1769476
  185.7 36.2 %copy-start.4 = (bf16[2,192,768]{2,1,0:T(8,128)(2,1)S(1)}, bf16[2,192,768]{2,1,0:T(8,128)(2,1)}, u32[]{:S(2)}) copy-start(bf16[2,192,768]{2,1,0:T(8,128)(2,1)} %get-tuple-element.55.refs_15_) | copy-start | bytes 1769476
  185.7 37.9 %copy-start.36 = (bf16[48,3072]{1,0:T(8,128)(2,1)S(1)}, bf16[48,3072]{1,0:T(8,128)(2,1)}, u32[]{:S(2)}) copy-start(bf16[48,3072]{1,0:T(8,128)(2,1)} %copy-done.35) | copy-start | bytes 884740
  185.7 67.2 %slice-start.1 = ((s8[6291456]{0:T(1024)(128)(4,1)}), s8[2097152]{0:T(1024)(128)(4,1)S(1)}, s32[]{:S(2)}) async-start(s8[6291456]{0:T(1024)(128)(4,1)} %bitcast.121), calls=%async_computation.5 | async-start | bytes 4194304
  188.4 63.1 %copy-start.27 = (bf16[4,192,192]{2,1,0:T(8,128)(2,1)}, bf16[4,192,192]{2,1,0:T(8,128)(2,1)S(1)}, u32[]{:S(2)}) copy-start(bf16[4,192,192]{2,1,0:T(8,128)(2,1)S(1)} %collective-permute-done.14.refs_5_) | copy-start | bytes 884740
  188.4 61.3 %collective-permute-start.24 = (bf16[2,192,768]{2,1,0:T(8,128)(2,1)}, bf16[2,192,768]{2,1,0:T(8,128)(2,1)S(1)}, u32[]{:S(2)}, u32[]{:S(2)}) collective-permute-start(bf16[2,192,768]{2,1,0:T(8,128)(2,1)} %get-tuple-element.52.refs_12_), channel_id=1, source_target_pairs={{0,8},{8,0},{16,24},{24,16},{1,9},{9,1},{17,25},{25,17},{2,10},{10... | collective-permute-start | bytes 1769480 | tf_op jit(solution)/shard_map/ppermute | solution.py:175
  213.8 37.8 %copy-start.28 = (bf16[4,192,192]{2,1,0:T(8,128)(2,1)}, bf16[4,192,192]{2,1,0:T(8,128)(2,1)S(1)}, u32[]{:S(2)}) copy-start(bf16[4,192,192]{2,1,0:T(8,128)(2,1)S(1)} %collective-permute-done.15.refs_6_) | copy-start | bytes 884740
  213.8 36.5 %collective-permute-start.25 = (bf16[2,192,768]{2,1,0:T(8,128)(2,1)}, bf16[2,192,768]{2,1,0:T(8,128)(2,1)S(1)}, u32[]{:S(2)}, u32[]{:S(2)}) collective-permute-start(bf16[2,192,768]{2,1,0:T(8,128)(2,1)} %get-tuple-element.53.refs_13_), channel_id=1, source_target_pairs={{0,8},{8,0},{16,24},{24,16},{1,9},{9,1},{17,25},{25,17},{2,10},{10... | collective-permute-start | bytes 1769480 | tf_op jit(solution)/shard_map/ppermute | solution.py:175
  221.2 30.4 %copy-start.29 = (bf16[4,192,192]{2,1,0:T(8,128)(2,1)}, bf16[4,192,192]{2,1,0:T(8,128)(2,1)S(1)}, u32[]{:S(2)}) copy-start(bf16[4,192,192]{2,1,0:T(8,128)(2,1)S(1)} %collective-permute-done.16.refs_7_) | copy-start | bytes 884740
  221.2 16.2 %collective-permute-start.22 = (bf16[2,192,768]{2,1,0:T(8,128)(2,1)S(1)}, bf16[2,192,768]{2,1,0:T(8,128)(2,1)S(1)}, u32[]{:S(2)}, u32[]{:S(2)}) collective-permute-start(bf16[2,192,768]{2,1,0:T(8,128)(2,1)S(1)} %copy-done.5), channel_id=1, source_target_pairs={{0,16},{8,24},{16,0},{24,8},{1,17},{9,25},{17,1},{25,9},{2,18},{10... | collective-permute-start | bytes 1769480 | tf_op jit(solution)/shard_map/ppermute | solution.py:175
  221.7 31.2 %copy-start.8 = (bf16[2,192,768]{2,1,0:T(8,128)(2,1)}, bf16[2,192,768]{2,1,0:T(8,128)(2,1)S(1)}, u32[]{:S(2)}) copy-start(bf16[2,192,768]{2,1,0:T(8,128)(2,1)S(1)} %collective-permute-done.20.refs_16_) | copy-start | bytes 1769476
  221.7 28.7 %collective-permute-start.26 = (bf16[2,192,768]{2,1,0:T(8,128)(2,1)S(1)}, bf16[2,192,768]{2,1,0:T(8,128)(2,1)S(1)}, u32[]{:S(2)}, u32[]{:S(2)}) collective-permute-start(bf16[2,192,768]{2,1,0:T(8,128)(2,1)S(1)} %copy-done.5), channel_id=1, source_target_pairs={{0,8},{8,0},{16,24},{24,16},{1,9},{9,1},{17,25},{25,17},{2,10},{10... | collective-permute-start | bytes 1769480 | tf_op jit(solution)/shard_map/ppermute | solution.py:175
  221.9 30.9 %copy-start.9 = (bf16[2,192,768]{2,1,0:T(8,128)(2,1)}, bf16[2,192,768]{2,1,0:T(8,128)(2,1)S(1)}, u32[]{:S(2)}) copy-start(bf16[2,192,768]{2,1,0:T(8,128)(2,1)S(1)} %collective-permute-done.21.refs_17_) | copy-start | bytes 1769476
  221.9 27.8 %collective-permute-start.23 = (bf16[2,192,768]{2,1,0:T(8,128)(2,1)S(1)}, bf16[2,192,768]{2,1,0:T(8,128)(2,1)S(1)}, u32[]{:S(2)}, u32[]{:S(2)}) collective-permute-start(bf16[2,192,768]{2,1,0:T(8,128)(2,1)S(1)} %copy-done.4), channel_id=1, source_target_pairs={{0,16},{8,24},{16,0},{24,8},{1,17},{9,25},{17,1},{25,9},{2,18},{10... | collective-permute-start | bytes 1769480 | tf_op jit(solution)/shard_map/ppermute | solution.py:175
  237.4 18.3 %collective-permute-start.27 = (bf16[2,192,768]{2,1,0:T(8,128)(2,1)S(1)}, bf16[2,192,768]{2,1,0:T(8,128)(2,1)S(1)}, u32[]{:S(2)}, u32[]{:S(2)}) collective-permute-start(bf16[2,192,768]{2,1,0:T(8,128)(2,1)S(1)} %copy-done.4), channel_id=1, source_target_pairs={{0,8},{8,0},{16,24},{24,16},{1,9},{9,1},{17,25},{25,17},{2,10},{10... | collective-permute-start | bytes 1769480 | tf_op jit(solution)/shard_map/ppermute | solution.py:175
  249.7 6.0 %collective-permute-start.28 = (bf16[2,192,768]{2,1,0:T(8,128)(2,1)S(1)}, bf16[2,192,768]{2,1,0:T(8,128)(2,1)S(1)}, u32[]{:S(2)}, u32[]{:S(2)}) collective-permute-start(bf16[2,192,768]{2,1,0:T(8,128)(2,1)S(1)} %collective-permute-done.20.refs_16_), channel_id=1, source_target_pairs={{0,8},{8,0},{16,24},{24,16},{1,9},{9,1},{17,25},{25,17},{2,10},{10... | collective-permute-start | bytes 1769480 | tf_op jit(solution)/shard_map/ppermute | solution.py:175
  249.7 6.0 %collective-permute-start.29 = (bf16[2,192,768]{2,1,0:T(8,128)(2,1)S(1)}, bf16[2,192,768]{2,1,0:T(8,128)(2,1)S(1)}, u32[]{:S(2)}, u32[]{:S(2)}) collective-permute-start(bf16[2,192,768]{2,1,0:T(8,128)(2,1)S(1)} %collective-permute-done.21.refs_17_), channel_id=1, source_target_pairs={{0,8},{8,0},{16,24},{24,16},{1,9},{9,1},{17,25},{25,17},{2,10},{10... | collective-permute-start | bytes 1769480 | tf_op jit(solution)/shard_map/ppermute | solution.py:175
  250.2 5.5 %collective-permute-start.30 = (bf16[2,192,768]{2,1,0:T(8,128)(2,1)S(1)}, bf16[2,192,768]{2,1,0:T(8,128)(2,1)S(1)}, u32[]{:S(2)}, u32[]{:S(2)}) collective-permute-start(bf16[2,192,768]{2,1,0:T(8,128)(2,1)S(1)} %collective-permute-done.22.refs_18_), channel_id=1, source_target_pairs={{0,8},{8,0},{16,24},{24,16},{1,9},{9,1},{17,25},{25,17},{2,10},{10... | collective-permute-start | bytes 1769480 | tf_op jit(solution)/shard_map/ppermute | solution.py:175
  251.2 4.6 %collective-permute-start.31 = (bf16[2,192,768]{2,1,0:T(8,128)(2,1)S(1)}, bf16[2,192,768]{2,1,0:T(8,128)(2,1)S(1)}, u32[]{:S(2)}, u32[]{:S(2)}) collective-permute-start(bf16[2,192,768]{2,1,0:T(8,128)(2,1)S(1)} %collective-permute-done.23.refs_19_), channel_id=1, source_target_pairs={{0,8},{8,0},{16,24},{24,16},{1,9},{9,1},{17,25},{25,17},{2,10},{10... | collective-permute-start | bytes 1769480 | tf_op jit(solution)/shard_map/ppermute | solution.py:175
  (35 other events, 280.5 us)
Sparse Core Ops, SparseCore 0:
  34.2 31.3 all-gather.4
  67.1 30.7 all-gather.2

commit v3 on v2

--- a/solution.py
+++ b/solution.py
@@ -106,61 +106,64 @@
     )(me, rows)
 
 
-def weight_kernel(n_groups, halves, chunks, *refs):
-    rows = refs[: n_groups * halves]
-    refs = refs[n_groups * halves :]
-    lows = refs[:n_groups]
-    grads = refs[n_groups : n_groups + n_groups * chunks]
-    block_out, low_out = refs[n_groups + n_groups * chunks :]
-    n_blocks = block_out.shape[1]
-    per_chunk = n_blocks // chunks
-    per_half = n_blocks // halves
-    for b in range(n_blocks):
-        block_sum = None
-        low_sum = None
-        for g in range(n_groups):
-            grad = grads[g * chunks + b // per_chunk][b % per_chunk]
-            row = rows[g * halves + b // per_half][b % per_half]
-            block_part = dot(row, grad, 0, 0)
-            low_part = dot(lows[g][...], grad, 0, 0)
-            block_sum = block_part if g == 0 else block_sum + block_part
-            low_sum = low_part if g == 0 else low_sum + low_part
-        block_out[:, b, :] = block_sum
-        low_out[:, b, :] = low_sum
-
-
-def weight_grads(rows, lows, grads):
+def weight_kernel(n_groups, chunks, ready, *refs):
+    rows = refs[:n_groups]
+    lows = refs[n_groups : 2 * n_groups]
+    refs = refs[2 * n_groups :]
+    grads = refs[: n_groups * chunks]
+    done = refs[n_groups * chunks : -2]
+    block_out, low_out = refs[-2:]
+    per_chunk = grads[0].shape[0]
+    low_all = jnp.concatenate([x[...] for x in lows], axis=0)
+    for b in range(ready):
+        block_out[:, b, :] = done[0][b]
+        low_out[:, b, :] = done[1][b]
+    for b in range(per_chunk * chunks):
+        grad = jnp.concatenate(
+            [grads[g * chunks + b // per_chunk][b % per_chunk] for g in range(n_groups)], axis=0
+        )
+        row = jnp.concatenate([x[b] for x in rows], axis=0)
+        block_sum = dot(row, grad, 0, 0)
+        low_sum = dot(low_all, grad, 0, 0)
+        if done:
+            block_out[:, ready + b, :] = block_sum
+            low_out[:, ready + b, :] = low_sum
+        else:
+            block_out[b] = block_sum
+            low_out[b] = low_sum
+
+
+def weight_grads(rows, lows, grads, done=()):
     n_groups = len(rows)
-    halves = len(rows[0])
     chunks = len(grads[0])
-    per_half, tokens, part = rows[0][0].shape
+    count, tokens, part = rows[0].shape
     per_chunk, _, width = grads[0][0].shape
-    n_blocks = per_chunk * chunks
     rank = lows[0].shape[1]
     tile = 256 if width % 256 == 0 else width
-    flat_rows = [x for group in rows for x in group]
     flat_grads = [x for group in grads for x in group]
+    ready = done[0].shape[0] if done else 0
+    if done:
+        shapes = [(part, ready + count, width), (rank, ready + count, width)]
+        blocks = [(part, ready + count, tile), (rank, ready + count, tile)]
+    else:
+        shapes = [(count, part, width), (count, rank, width)]
+        blocks = [(count, part, tile), (count, rank, tile)]
     return pl.pallas_call(
-        functools.partial(weight_kernel, n_groups, halves, chunks),
+        functools.partial(weight_kernel, n_groups, chunks, ready),
         grid=(width // tile,),
-        in_specs=[pl.BlockSpec((per_half, tokens, part), lambda j: (0, 0, 0))] * len(flat_rows)
+        in_specs=[pl.BlockSpec((count, tokens, part), lambda j: (0, 0, 0))] * n_groups
         + [pl.BlockSpec((tokens, rank), lambda j: (0, 0))] * n_groups
-        + [pl.BlockSpec((per_chunk, tokens, tile), lambda j: (0, 0, j))] * len(flat_grads),
-        out_specs=[
-            pl.BlockSpec((part, n_blocks, tile), lambda j: (0, 0, j)),
-            pl.BlockSpec((rank, n_blocks, tile), lambda j: (0, 0, j)),
-        ],
-        out_shape=[
-            jax.ShapeDtypeStruct((part, n_blocks, width), F32),
-            jax.ShapeDtypeStruct((rank, n_blocks, width), F32),
-        ],
+        + [pl.BlockSpec((per_chunk, tokens, tile), lambda j: (0, 0, j))] * len(flat_grads)
+        + [pl.BlockSpec((ready, x.shape[1], tile), lambda j: (0, 0, j)) for x in done],
+        out_specs=[pl.BlockSpec(x, lambda j: (0, 0, j)) for x in blocks],
+        out_shape=[jax.ShapeDtypeStruct(x, F32) for x in shapes],
         cost_estimate=pl.CostEstimate(
-            flops=2 * n_groups * tokens * n_blocks * width * (part + rank),
-            bytes_accessed=2 * n_groups * tokens * n_blocks * width
-            + 4 * (part + rank) * n_blocks * width,
+            flops=2 * n_groups * tokens * count * width * (part + rank),
+            bytes_accessed=2 * n_groups * tokens * count * width
+            + 4 * (part + rank) * (count + 2 * ready) * width,
             transcendentals=0,
         ),
-    )(*flat_rows, *lows, *flat_grads)
+    )(*rows, *lows, *flat_grads, *done)
 
 
 def doc_weights(segment_row, alive_count):
@@ -190,6 +193,19 @@
             arrived.append(swap(x, "dp", mask))
         held = held + arrived
     return held
+
+
+def col_gather(own, direct):
+    if not direct:
+        return lax.all_gather(own, "col", axis=0, tiled=True)
+    n_col = lax.axis_size("col")
+    me = lax.axis_index("col")
+    size = own.shape[0]
+    full = jnp.zeros((n_col * size, own.shape[1]), own.dtype)
+    for k in range(n_col):
+        piece = swap(own, "col", k) if k else own
+        full = lax.dynamic_update_slice(full, piece, ((me ^ k) * size, 0))
+    return full
 
 
 def col_total(part, direct):
@@ -230,28 +246,32 @@
     flat_index = sender * capacity + offset
     my_rows = jnp.take(incoming.reshape(n_data * capacity, incoming.shape[2]), flat_index, axis=0)
 
-    segment_row, _ = lax.optimization_barrier((segments[0], my_rows))
+    flat_in = lowrank_in.reshape(n_blocks * block_in, rank_width)
+    own_part = jnp.dot(my_rows, flat_in, preferred_element_type=F32).astype(BF16)
+    segment_row, own_part, later_rows = lax.optimization_barrier((segments[0], own_part, my_rows))
+    own_low = row_total(own_part).astype(BF16)
     my_alive = jnp.sum(lax.dynamic_index_in_dim(count_table, my_data, 0, keepdims=False))
     weights = doc_weights(segment_row, my_alive)
     out_weights = jnp.take(weights, slot_table, axis=0)
     in_weights = lax.all_to_all(out_weights, "dp", split_axis=0, concat_axis=0, tiled=True)
     my_weights = jnp.take(in_weights.reshape(n_data * capacity), flat_index, axis=0)
-
-    flat_in = lowrank_in.reshape(n_blocks * block_in, rank_width)
-    own_part = jnp.dot(my_rows, flat_in, preferred_element_type=F32)
-    own_low = row_total(own_part).astype(BF16)
     own_extra = jnp.concatenate(
         [own_low, jnp.broadcast_to(my_weights[:, None], (own_rows, 128))], axis=1
     )
+    direct = n_col <= 4
+    if direct:
+        lowrank_out, cotangent, own_extra = lax.optimization_barrier(
+            (lowrank_out, cotangent, own_extra)
+        )
     halves = 2
     half_width = n_blocks * block_in // halves
     panel_low = None
     panels = []
     for h in range(halves):
-        piece = my_rows[:, h * half_width : (h + 1) * half_width]
+        piece = (later_rows if h else my_rows)[:, h * half_width : (h + 1) * half_width]
         panels.append(lax.all_gather(piece, "col", axis=0, tiled=True))
         if h == 0:
-            extra = lax.all_gather(own_extra, "col", axis=0, tiled=True)
+            extra = col_gather(own_extra, direct)
             panel_low = extra[:, :rank_width]
             tok_weight = extra[:, rank_width : rank_width + 1].astype(F32)
 
@@ -273,7 +293,6 @@
     per_chunk = n_blocks // chunks
     acts, grads, in_terms, low_terms, row_parts = [], [], [], [], []
     me_array = jnp.full((1,), my_data, jnp.int32)
-    direct = n_col <= 4
     group_slices = [[] for _ in offsets]
     for h in range(halves):
         row_parts.append(split_rows(me_array, panels[h], per_half, offsets))
@@ -313,8 +332,14 @@
     input_grad = (own_term + dot(low_grad, flat_in, 1, 1)).astype(BF16)
 
     act_out = jnp.transpose(jnp.concatenate(acts, axis=0), (1, 0, 2))
-    by_group = [[grads[c][g] for c in range(chunks)] for g in range(n_data)]
-    block_grad, out_grad = weight_grads(group_slices, group_lows, by_group)
+    done = ()
+    for h in range(halves):
+        by_group = [
+            [grads[c][g] for c in range(h * half_chunks, (h + 1) * half_chunks)]
+            for g in range(n_data)
+        ]
+        done = weight_grads([x[h] for x in group_slices], group_lows, by_group, done)
+    block_grad, out_grad = done
     return (act_out, input_grad, block_grad, out_grad)
 
 

time: 277 us -> 284 us (1.025)
  blocking collectives: 15.2 us -> 0 us
  waiting for transfers between devices: 104 us -> 117 us
  Pallas kernels: 44.5 us -> 50.4 us
    all_gather x2, waiting for transfers between devices: 7.47 us -> 24.4 us  [local(): panels.append(lax.all_gather(piece, 'col', axis=0, tiled=True))]
    all_gather x1 -> x0, blocking collectives: 15.2 us -> none  [local(): extra = lax.all_gather(own_extra, 'col', axis=0, tiled=True)]
    optimization_barrier x0 -> x2, local copies, waits for them, and re-layouts: none -> 8.69 us  [local(): lax.optimization_barrier((lowrank_out, cotangent, own_extra))]
    unnamed x101 -> x81, local copies, waits for them, and re-layouts: 16.8 us -> 8.42 us
    pallas_call x1 -> x2, Pallas kernels: 11.7 us -> 17.7 us  [weight_grads(): pl.pallas_call(functools.partial(weight_kernel, n_groups, chunks, ready),...]
    ppermute x32 -> x35, waiting for transfers between devices: 87 us -> 81.7 us  [swap(): lax.ppermute(value, axis, [(s, s ^ mask) for s in range(lax.axis_size(axi...]
    ppermute x32 -> x35, starting transfers between devices: 37.3 us -> 39.5 us  [swap(): lax.ppermute(value, axis, [(s, s ^ mask) for s in range(lax.axis_size(axi...]
  transfers between devices with their start and end apart: 36 -> 39, of which waited for: 11 -> 14; matrix products, arithmetic and copies ran while one was open for 15% -> 14% of each run, Pallas kernels for 12% -> 14%
where the time goes in v3:
time: 284 us; the launch traced here: 283 us
  waiting for transfers between devices  117 us (41%)
  Pallas kernels  50.4 us (18%)
  starting transfers between devices  47.4 us (17%)
  local copies, waits for them, and re-layouts  28.4 us (10%)
  other arithmetic  19.1 us (7%)
  between operations  14.6 us (5%)
  matrix products  6.72 us (2%)
    ppermute x35, waiting for transfers between devices, swap(): lax.ppermute(value, axis, [(s, s ^ mask) for s in range(lax.axis_size(axi...  81.7 us
    ppermute x35, starting transfers between devices, swap(): lax.ppermute(value, axis, [(s, s ^ mask) for s in range(lax.axis_size(axi...  39.5 us
    pallas_call x4, Pallas kernels, block_chunk(): pl.pallas_call(block_kernel, grid=(count,), in_specs=[pl.BlockSpec((token...  24.7 us
    all_gather x2, waiting for transfers between devices, local(): panels.append(lax.all_gather(piece, 'col', axis=0, tiled=True))  24.4 us
    pallas_call x2, Pallas kernels, weight_grads(): pl.pallas_call(functools.partial(weight_kernel, n_groups, chunks, ready),...  17.7 us
    all_to_all x1, waiting for transfers between devices, local(): lax.all_to_all(outgoing, 'dp', split_axis=0, concat_axis=0, tiled=True)  9.5 us
    optimization_barrier x2, local copies, waits for them, and re-layouts, local(): lax.optimization_barrier((lowrank_out, cotangent, own_extra))  8.69 us
    unnamed x81, local copies, waits for them, and re-layouts  8.42 us
  transfers between devices with their start and end apart: 39, of which 14 were waited for; matrix products, arithmetic and copies ran while one was open for 14% of the time, Pallas kernels for 14%

profile of v3, /device:TPU:0, one launch (start us, length us, event | category | flops | bytes accessed | tf_op | source)
XLA Modules:
  0.0 283.3 jit_solution(9712290858132178136)
XLA Ops:
  8.7 1.2 gather_fusion
  11.5 4.4 %all-to-all-start = ((bf16[4,23,6144]{2,1,0:T(8,128)(2,1)}), bf16[4,23,6144]{2,1,0:T(8,128)(2,1)S(1)}, u32[]{:S(2)}, u32[]{:S(2)}) async-start(bf16[4,23,6144]{2,1,0:T(8,128)(2,1)} %broadcast_select_fusion), calls=%async_computation | async-start | bytes 2359296 | tf_op jit(solution)/shard_map/all_to_all | solution.py:239
  17.0 2.6 fusion.12
  19.7 2.6 compare_and_fusion.1
  22.3 9.5 %all-to-all-done = bf16[4,23,6144]{2,1,0:T(8,128)(2,1)S(1)} async-done(((bf16[4,23,6144]{2,1,0:T(8,128)(2,1)}), bf16[4,23,6144]{2,1,0:T(8,128)(2,1)S(1)}, u32[]{:S(2)}, u32[]{:S(2)}) %all-to-all-start) | async-done | bytes 1130528 | tf_op jit(solution)/shard_map/all_to_all | solution.py:239
  33.2 4.0 %convolution_convert_fusion = bf16[48,512]{1,0:T(8,128)(2,1)S(1)} fusion(bf16[48,6144]{1,0:T(8,128)(2,1)S(1)} %broadcast_select_fusion.1, bf16[6144,512]{1,0:T(8,128)(2,1)} %bitcast.120), kind=kOutput, calls=%fused_computation.12 | convolution fusion | flops 302014464 | bytes 6930432 | tf_op jit(solution)/shard_map/dot_general | solution.py:250
  40.2 1.2 gather_fusion.2
  42.1 3.4 %all-to-all-start.1 = ((bf16[4,1,23]{2,1,0:T(2,128)(2,1)}), bf16[4,1,23]{2,1,0:T(2,128)(2,1)S(1)}, u32[]{:S(2)}, u32[]{:S(2)}) async-start(bf16[4,1,23]{2,1,0:T(2,128)(2,1)} %copy.42), calls=%async_computation.1 | async-start | bytes 4096 | tf_op jit(solution)/shard_map/all_to_all | solution.py:256
  45.5 2.3 collective-permute-start
  47.8 1.2 all-to-all-done.1
  49.9 2.6 broadcast_select_fusion.2
  52.6 2.4 collective-permute-start.1
  55.0 2.6 collective-permute-start.2
  57.6 6.8 %copy.60 = bf16[512,8,768]{2,0,1:T(8,128)(2,1)} copy(bf16[512,8,768]{2,1,0:T(8,128)(2,1)} %param.14) | data formatting | bytes 12582912 | tf_op jit(solution)/shard_map/optimization_barrier | solution.py:263
  64.4 1.9 copy.61
  68.9 6.0 %all-gather.5.cloned.1.call-done.rows = bf16[192,3072]{1,0:T(8,128)(2,1)} async-done(((bf16[48,3072]{1,0:T(8,128)(2,1)}), bf16[192,3072]{1,0:T(8,128)(2,1)}) %all-gather.5.cloned.1.call-update) | async-done | bytes 1179664 | tf_op jit(solution)/shard_map/all_gather | solution.py:272
  74.9 6.1 %shard_map.114 = (bf16[2,192,768]{2,1,0:T(8,128)(2,1)}, bf16[2,192,768]{2,1,0:T(8,128)(2,1)}, bf16[192,1536]{1,0:T(8,128)(2,1)}, f32[192,512]{1,0:T(8,128)}) custom-call(bf16[192,3072]{1,0:T(8,128)(2,1)} %all-gather.5.cloned.1.call-done.rows, bf16[8,768,768]{2,1,0:T(8,128)(2,1)} %weight.7, bf16[192,512]{1,0:T(8,128)(2,1)} %copy-done.2, ...), custom_call_target="tpu_custom_call" | custom-call | flops 1509949440 | bytes 5701632 | tf_op jit(solution)/shard_map/pallas_call | solution.py:48
  81.0 6.2 %shard_map.113 = (bf16[2,192,768]{2,1,0:T(8,128)(2,1)}, bf16[2,192,768]{2,1,0:T(8,128)(2,1)}, bf16[192,1536]{1,0:T(8,128)(2,1)}, f32[192,512]{1,0:T(8,128)}) custom-call(bf16[192,3072]{1,0:T(8,128)(2,1)} %all-gather.5.cloned.1.call-done.rows, bf16[8,768,768]{2,1,0:T(8,128)(2,1)} %weight.7, bf16[192,512]{1,0:T(8,128)(2,1)} %copy-done.2, ...), custom_call_target="tpu_custom_call" | custom-call | flops 1509949440 | bytes 5701632 | tf_op jit(solution)/shard_map/pallas_call | solution.py:48
  87.2 18.4 %all-gather.3.cloned.1.call-done.rows = bf16[192,3072]{1,0:T(8,128)(2,1)} async-done(((bf16[48,3072]{1,0:T(8,128)(2,1)}), bf16[192,3072]{1,0:T(8,128)(2,1)}) %all-gather.3.cloned.1.call-update) | async-done | bytes 1179664 | tf_op jit(solution)/shard_map/all_gather | solution.py:272
  105.6 6.2 %shard_map.112 = (bf16[2,192,768]{2,1,0:T(8,128)(2,1)}, bf16[2,192,768]{2,1,0:T(8,128)(2,1)}, bf16[192,1536]{1,0:T(8,128)(2,1)}, f32[192,512]{1,0:T(8,128)}) custom-call(bf16[192,3072]{1,0:T(8,128)(2,1)} %all-gather.3.cloned.1.call-done.rows, bf16[8,768,768]{2,1,0:T(8,128)(2,1)} %weight.7, bf16[192,512]{1,0:T(8,128)(2,1)} %copy-done.2, ...), custom_call_target="tpu_custom_call" | custom-call | flops 1509949440 | bytes 5701632 | tf_op jit(solution)/shard_map/pallas_call | solution.py:48
  111.8 6.2 %shard_map.111 = (bf16[2,192,768]{2,1,0:T(8,128)(2,1)}, bf16[2,192,768]{2,1,0:T(8,128)(2,1)}, bf16[192,1536]{1,0:T(8,128)(2,1)}, f32[192,512]{1,0:T(8,128)}) custom-call(bf16[192,3072]{1,0:T(8,128)(2,1)} %all-gather.3.cloned.1.call-done.rows, bf16[8,768,768]{2,1,0:T(8,128)(2,1)} %weight.7, bf16[192,512]{1,0:T(8,128)(2,1)} %copy-done.2, ...), custom_call_target="tpu_custom_call" | custom-call | flops 1509949440 | bytes 5701632 | tf_op jit(solution)/shard_map/pallas_call | solution.py:48
  118.1 1.2 add_convert_fusion
  119.3 1.7 collective-permute-start.12
  122.1 1.7 collective-permute-start.10
  126.8 2.0 collective-permute-start.9
  128.9 2.4 collective-permute-start.7
  131.4 1.5 collective-permute-start.13
  133.8 2.2 collective-permute-start.6
  136.7 4.0 %shard_map.115 = (bf16[4,192,192]{2,1,0:T(8,128)(2,1)}, bf16[4,192,192]{2,1,0:T(8,128)(2,1)}, bf16[4,192,192]{2,1,0:T(8,128)(2,1)}, bf16[4,192,192]{2,1,0:T(8,128)(2,1)}) custom-call(s32[1]{0:T(128)} %bitcast.32.me, bf16[192,3072]{1,0:T(8,128)(2,1)} %all-gather.5.cloned.1.call-done.rows), custom_call_target="tpu_custom_call" | custom-call | bytes 2359296 | tf_op jit(solution)/shard_map/pallas_call | solution.py:94
  140.6 8.9 %collective-permute-start.4 = (bf16[48,3072]{1,0:T(8,128)(2,1)}, bf16[48,3072]{1,0:T(8,128)(2,1)}, u32[]{:S(2)}, u32[]{:S(2)}) collective-permute-start(bf16[48,3072]{1,0:T(8,128)(2,1)} %get-tuple-element.92), channel_id=1, source_target_pairs={{0,1},{1,0},{2,3},{3,2},{4,5},{5,4},{6,7},{7,6},{8,9},{9,8},{10,11... | collective-permute-start | bytes 884744 | tf_op jit(solution)/shard_map/ppermute | solution.py:178
  149.6 18.4 %collective-permute-done.8 = bf16[48,3072]{1,0:T(8,128)(2,1)} collective-permute-done((bf16[48,3072]{1,0:T(8,128)(2,1)}, bf16[48,3072]{1,0:T(8,128)(2,1)}, u32[]{:S(2)}, u32[]{:S(2)}) %collective-permute-start.8) | collective-permute-done | bytes 294944 | tf_op jit(solution)/shard_map/ppermute | solution.py:178
  168.0 1.8 collective-permute-start.14
  170.1 10.5 %collective-permute-done.5 = bf16[48,3072]{1,0:T(8,128)(2,1)} collective-permute-done((bf16[48,3072]{1,0:T(8,128)(2,1)}, bf16[48,3072]{1,0:T(8,128)(2,1)}, u32[]{:S(2)}, u32[]{:S(2)}) %collective-permute-start.5) | collective-permute-done | bytes 294944 | tf_op jit(solution)/shard_map/ppermute | solution.py:178
  181.6 4.0 %shard_map.116 = (bf16[4,192,192]{2,1,0:T(8,128)(2,1)}, bf16[4,192,192]{2,1,0:T(8,128)(2,1)}, bf16[4,192,192]{2,1,0:T(8,128)(2,1)}, bf16[4,192,192]{2,1,0:T(8,128)(2,1)}) custom-call(s32[1]{0:T(128)} %bitcast.32.me, bf16[192,3072]{1,0:T(8,128)(2,1)} %all-gather.3.cloned.1.call-done.rows), custom_call_target="tpu_custom_call" | custom-call | bytes 2359296 | tf_op jit(solution)/shard_map/pallas_call | solution.py:94
  187.8 1.5 copy.65
  189.3 1.9 maximum_bitcast_fusion
  191.2 2.7 copy.49
  193.9 20.0 %collective-permute-done.26.refs_1_ = bf16[4,192,192]{2,1,0:T(8,128)(2,1)S(1)} collective-permute-done((bf16[4,192,192]{2,1,0:T(8,128)(2,1)}, bf16[4,192,192]{2,1,0:T(8,128)(2,1)S(1)}, u32[]{:S(2)}, u32[]{:S(2)}) %collective-permute-start.26) | collective-permute-done | bytes 294944 | tf_op jit(solution)/shard_map/ppermute | solution.py:178
  213.9 1.8 collective-permute-start.30
  215.7 6.0 %collective-permute-done.28.refs_3_ = bf16[4,192,192]{2,1,0:T(8,128)(2,1)S(1)} collective-permute-done((bf16[4,192,192]{2,1,0:T(8,128)(2,1)}, bf16[4,192,192]{2,1,0:T(8,128)(2,1)S(1)}, u32[]{:S(2)}, u32[]{:S(2)}) %collective-permute-start.28) | collective-permute-done | bytes 294944 | tf_op jit(solution)/shard_map/ppermute | solution.py:178
  222.1 1.8 collective-permute-start.21
  223.9 1.3 fusion.2
  225.2 21.7 %collective-permute-done.21.refs_11_ = bf16[2,192,768]{2,1,0:T(8,128)(2,1)} collective-permute-done((bf16[2,192,768]{2,1,0:T(8,128)(2,1)S(1)}, bf16[2,192,768]{2,1,0:T(8,128)(2,1)}, u32[]{:S(2)}, u32[]{:S(2)}) %collective-permute-start.21) | collective-permute-done | bytes 589856 | tf_op jit(solution)/shard_map/ppermute | solution.py:178
  248.1 1.4 fusion.4
  249.5 2.8 collective-permute-done.34.refs_15_
  253.2 2.8 fusion
  256.0 7.3 %shard_map.117 = (f32[4,192,768]{2,1,0:T(8,128)}, f32[4,128,768]{2,1,0:T(8,128)}) custom-call(bf16[4,192,192]{2,1,0:T(8,128)(2,1)} %get-tuple-element.62.refs_0_, bf16[4,192,192]{2,1,0:T(8,128)(2,1)} %copy-done.20, bf16[4,192,192]{2,1,0:T(8,128)(2,1)} %copy-done.21, bf16[4,192,192]{2,1,0:T(8,128)(2,1)} %copy-done.22, bf16[192,128]{1,0:T(8,128)(2,1)} %bitcast.130, ...), custom_call_target="tpu_custom_call" | custom-call | flops 1509949440 | bytes 8650752 | tf_op jit(solution)/shard_map/pallas_call | solution.py:151
  266.1 10.4 %shard_map.118 = (f32[192,8,768]{2,1,0:T(8,128)}, f32[128,8,768]{2,1,0:T(8,128)}) custom-call(bf16[4,192,192]{2,1,0:T(8,128)(2,1)} %get-tuple-element.56.refs_0_, bf16[4,192,192]{2,1,0:T(8,128)(2,1)} %collective-permute-done.14.refs_1_, bf16[4,192,192]{2,1,0:T(8,128)(2,1)} %collective-permute-done.15.refs_2_, bf16[4,192,192]{2,1,0:T(8,128)(2,1)} %copy-done.19, ...), custom_call_target="tpu_custom_call" | custom-call | flops 1509949440 | bytes 16515072 | tf_op jit(solution)/shard_map/pallas_call | solution.py:151
  (180 shorter events, 27.4 us)
Async XLA Ops:
  11.5 20.2 %all-to-all-start = ((bf16[4,23,6144]{2,1,0:T(8,128)(2,1)}), bf16[4,23,6144]{2,1,0:T(8,128)(2,1)S(1)}, u32[]{:S(2)}, u32[]{:S(2)}) async-start(bf16[4,23,6144]{2,1,0:T(8,128)(2,1)} %broadcast_select_fusion), calls=%async_computation | async-start | bytes 2359296 | tf_op jit(solution)/shard_map/all_to_all | solution.py:239
  15.9 59.0 %all-gather.5.cloned.1.call-start = ((), (), s32[]{:S(2)}) async-start(), calls=%async_computation.3 | async-start | bytes 1474560 | tf_op jit(solution)/shard_map/all_gather | solution.py:272
  37.9 67.7 %all-gather.3.cloned.1.call-start = ((), (), s32[]{:S(2)}) async-start(), calls=%async_computation.2 | async-start | bytes 1474560 | tf_op jit(solution)/shard_map/all_gather | solution.py:272
  42.1 6.9 %all-to-all-start.1 = ((bf16[4,1,23]{2,1,0:T(2,128)(2,1)}), bf16[4,1,23]{2,1,0:T(2,128)(2,1)S(1)}, u32[]{:S(2)}, u32[]{:S(2)}) async-start(bf16[4,1,23]{2,1,0:T(2,128)(2,1)} %copy.42), calls=%async_computation.1 | async-start | bytes 4096 | tf_op jit(solution)/shard_map/all_to_all | solution.py:256
  45.5 7.0 %collective-permute-start = (bf16[48,512]{1,0:T(8,128)(2,1)S(1)}, bf16[48,512]{1,0:T(8,128)(2,1)S(1)}, u32[]{:S(2)}, u32[]{:S(2)}) collective-permute-start(bf16[48,512]{1,0:T(8,128)(2,1)S(1)} %convolution_convert_fusion), channel_id=1, source_target_pairs={{0,4},{4,0},{1,5},{5,1},{2,6},{6,2},{3,7},{7,3},{8,12},{12,8},{9,1... | collective-permute-start | bytes 147464 | tf_op jit(solution)/shard_map/ppermute | solution.py:178
  52.6 13.7 %collective-permute-start.1 = (bf16[48,640]{1,0:T(8,128)(2,1)S(1)}, bf16[48,640]{1,0:T(8,128)(2,1)S(1)}, u32[]{:S(2)}, u32[]{:S(2)}) collective-permute-start(bf16[48,640]{1,0:T(8,128)(2,1)S(1)} %pad_maximum_fusion.2), channel_id=1, source_target_pairs={{0,1},{1,0},{2,3},{3,2},{4,5},{5,4},{6,7},{7,6},{8,9},{9,8},{10,11... | collective-permute-start | bytes 184328 | tf_op jit(solution)/shard_map/ppermute | solution.py:178
  55.0 11.5 %collective-permute-start.2 = (bf16[48,640]{1,0:T(8,128)(2,1)S(1)}, bf16[48,640]{1,0:T(8,128)(2,1)S(1)}, u32[]{:S(2)}, u32[]{:S(2)}) collective-permute-start(bf16[48,640]{1,0:T(8,128)(2,1)S(1)} %pad_maximum_fusion.2), channel_id=1, source_target_pairs={{0,2},{1,3},{2,0},{3,1},{4,6},{5,7},{6,4},{7,5},{8,10},{9,11},{10,... | collective-permute-start | bytes 184328 | tf_op jit(solution)/shard_map/ppermute | solution.py:178
  57.6 9.1 %collective-permute-start.3 = (bf16[48,640]{1,0:T(8,128)(2,1)S(1)}, bf16[48,640]{1,0:T(8,128)(2,1)S(1)}, u32[]{:S(2)}, u32[]{:S(2)}) collective-permute-start(bf16[48,640]{1,0:T(8,128)(2,1)S(1)} %pad_maximum_fusion.2), channel_id=1, source_target_pairs={{0,3},{1,2},{2,1},{3,0},{4,7},{5,6},{6,5},{7,4},{8,11},{9,10},{10,... | collective-permute-start | bytes 184328 | tf_op jit(solution)/shard_map/ppermute | solution.py:178
  67.9 61.0 %collective-permute-start.17 = (bf16[192,128]{1,0:T(8,128)(2,1)S(1)}, bf16[192,128]{1,0:T(8,128)(2,1)S(1)}, u32[]{:S(2)}, u32[]{:S(2)}) collective-permute-start(bf16[192,128]{1,0:T(8,128)(2,1)S(1)} %bitcast.134), channel_id=1, source_target_pairs={{0,16},{8,24},{16,0},{24,8},{1,17},{9,25},{17,1},{25,9},{2,18},{10... | collective-permute-start | bytes 147464 | tf_op jit(solution)/shard_map/ppermute | solution.py:178
  68.2 63.2 %collective-permute-start.18 = (bf16[192,128]{1,0:T(8,128)(2,1)S(1)}, bf16[192,128]{1,0:T(8,128)(2,1)S(1)}, u32[]{:S(2)}, u32[]{:S(2)}) collective-permute-start(bf16[192,128]{1,0:T(8,128)(2,1)S(1)} %bitcast.133), channel_id=1, source_target_pairs={{0,8},{8,0},{16,24},{24,16},{1,9},{9,1},{17,25},{25,17},{2,10},{10... | collective-permute-start | bytes 147464 | tf_op jit(solution)/shard_map/ppermute | solution.py:178
  119.3 6.8 %collective-permute-start.12 = (bf16[48,512]{1,0:T(8,128)(2,1)S(1)}, bf16[48,512]{1,0:T(8,128)(2,1)S(1)}, u32[]{:S(2)}, u32[]{:S(2)}) collective-permute-start(bf16[48,512]{1,0:T(8,128)(2,1)S(1)} %get-tuple-element.103), channel_id=1, source_target_pairs={{0,3},{1,2},{2,1},{3,0},{4,7},{5,6},{6,5},{7,4},{8,11},{9,10},{10,... | collective-permute-start | bytes 147464 | tf_op jit(solution)/shard_map/ppermute | solution.py:178
  121.0 5.8 %collective-permute-start.11 = (bf16[48,512]{1,0:T(8,128)(2,1)S(1)}, bf16[48,512]{1,0:T(8,128)(2,1)S(1)}, u32[]{:S(2)}, u32[]{:S(2)}) collective-permute-start(bf16[48,512]{1,0:T(8,128)(2,1)S(1)} %get-tuple-element.104), channel_id=1, source_target_pairs={{0,2},{1,3},{2,0},{3,1},{4,6},{5,7},{6,4},{7,5},{8,10},{9,11},{10,... | collective-permute-start | bytes 147464 | tf_op jit(solution)/shard_map/ppermute | solution.py:178
  122.1 6.8 %collective-permute-start.10 = (bf16[48,512]{1,0:T(8,128)(2,1)S(1)}, bf16[48,512]{1,0:T(8,128)(2,1)S(1)}, u32[]{:S(2)}, u32[]{:S(2)}) collective-permute-start(bf16[48,512]{1,0:T(8,128)(2,1)S(1)} %get-tuple-element.102), channel_id=1, source_target_pairs={{0,1},{1,0},{2,3},{3,2},{4,5},{5,4},{6,7},{7,6},{8,9},{9,8},{10,11... | collective-permute-start | bytes 147464 | tf_op jit(solution)/shard_map/ppermute | solution.py:178
  126.2 7.6 %collective-permute-start.19 = (bf16[192,128]{1,0:T(8,128)(2,1)S(1)}, bf16[192,128]{1,0:T(8,128)(2,1)S(1)}, u32[]{:S(2)}, u32[]{:S(2)}) collective-permute-start(bf16[192,128]{1,0:T(8,128)(2,1)S(1)} %bitcast.132), channel_id=1, source_target_pairs={{0,24},{8,16},{16,8},{24,0},{1,25},{9,17},{17,9},{25,1},{2,26},{10... | collective-permute-start | bytes 147464 | tf_op jit(solution)/shard_map/ppermute | solution.py:178
  126.8 13.8 %collective-permute-start.9 = (bf16[48,3072]{1,0:T(8,128)(2,1)}, bf16[48,3072]{1,0:T(8,128)(2,1)}, u32[]{:S(2)}, u32[]{:S(2)}) collective-permute-start(bf16[48,3072]{1,0:T(8,128)(2,1)} %get-tuple-element.96), channel_id=1, source_target_pairs={{0,3},{1,2},{2,1},{3,0},{4,7},{5,6},{6,5},{7,4},{8,11},{9,10},{10,... | collective-permute-start | bytes 884744 | tf_op jit(solution)/shard_map/ppermute | solution.py:178
  128.9 39.1 %collective-permute-start.8 = (bf16[48,3072]{1,0:T(8,128)(2,1)}, bf16[48,3072]{1,0:T(8,128)(2,1)}, u32[]{:S(2)}, u32[]{:S(2)}) collective-permute-start(bf16[48,3072]{1,0:T(8,128)(2,1)} %get-tuple-element.97), channel_id=1, source_target_pairs={{0,2},{1,3},{2,0},{3,1},{4,6},{5,7},{6,4},{7,5},{8,10},{9,11},{10,... | collective-permute-start | bytes 884744 | tf_op jit(solution)/shard_map/ppermute | solution.py:178
  128.9 40.8 %collective-permute-start.7 = (bf16[48,3072]{1,0:T(8,128)(2,1)}, bf16[48,3072]{1,0:T(8,128)(2,1)}, u32[]{:S(2)}, u32[]{:S(2)}) collective-permute-start(bf16[48,3072]{1,0:T(8,128)(2,1)} %get-tuple-element.95), channel_id=1, source_target_pairs={{0,1},{1,0},{2,3},{3,2},{4,5},{5,4},{6,7},{7,6},{8,9},{9,8},{10,11... | collective-permute-start | bytes 884744 | tf_op jit(solution)/shard_map/ppermute | solution.py:178
  131.4 4.7 %collective-permute-start.13 = (bf16[48,512]{1,0:T(8,128)(2,1)S(1)}, bf16[48,512]{1,0:T(8,128)(2,1)S(1)}, u32[]{:S(2)}, u32[]{:S(2)}) collective-permute-start(bf16[48,512]{1,0:T(8,128)(2,1)S(1)} %fusion.7), channel_id=1, source_target_pairs={{0,4},{4,0},{1,5},{5,1},{2,6},{6,2},{3,7},{7,3},{8,12},{12,8},{9,1... | collective-permute-start | bytes 147464 | tf_op jit(solution)/shard_map/ppermute | solution.py:178
  132.8 36.9 %copy-start.5 = (bf16[2,192,768]{2,1,0:T(8,128)(2,1)S(1)}, bf16[2,192,768]{2,1,0:T(8,128)(2,1)}, u32[]{:S(2)}) copy-start(bf16[2,192,768]{2,1,0:T(8,128)(2,1)} %get-tuple-element.60.refs_8_) | copy-start | bytes 1769476
  133.8 36.0 %collective-permute-start.6 = (bf16[48,3072]{1,0:T(8,128)(2,1)}, bf16[48,3072]{1,0:T(8,128)(2,1)}, u32[]{:S(2)}, u32[]{:S(2)}) collective-permute-start(bf16[48,3072]{1,0:T(8,128)(2,1)} %get-tuple-element.93), channel_id=1, source_target_pairs={{0,3},{1,2},{2,1},{3,0},{4,7},{5,6},{6,5},{7,4},{8,11},{9,10},{10,... | collective-permute-start | bytes 884744 | tf_op jit(solution)/shard_map/ppermute | solution.py:178
  136.0 44.6 %collective-permute-start.5 = (bf16[48,3072]{1,0:T(8,128)(2,1)}, bf16[48,3072]{1,0:T(8,128)(2,1)}, u32[]{:S(2)}, u32[]{:S(2)}) collective-permute-start(bf16[48,3072]{1,0:T(8,128)(2,1)} %get-tuple-element.94), channel_id=1, source_target_pairs={{0,2},{1,3},{2,0},{3,1},{4,6},{5,7},{6,4},{7,5},{8,10},{9,11},{10,... | collective-permute-start | bytes 884744 | tf_op jit(solution)/shard_map/ppermute | solution.py:178
  136.7 52.6 %copy-start.7 = (bf16[2,192,768]{2,1,0:T(8,128)(2,1)S(1)}, bf16[2,192,768]{2,1,0:T(8,128)(2,1)}, u32[]{:S(2)}) copy-start(bf16[2,192,768]{2,1,0:T(8,128)(2,1)} %get-tuple-element.47) | copy-start | bytes 1769476
  140.6 44.9 %collective-permute-start.4 = (bf16[48,3072]{1,0:T(8,128)(2,1)}, bf16[48,3072]{1,0:T(8,128)(2,1)}, u32[]{:S(2)}, u32[]{:S(2)}) collective-permute-start(bf16[48,3072]{1,0:T(8,128)(2,1)} %get-tuple-element.92), channel_id=1, source_target_pairs={{0,1},{1,0},{2,3},{3,2},{4,5},{5,4},{6,7},{7,6},{8,9},{9,8},{10,11... | collective-permute-start | bytes 884744 | tf_op jit(solution)/shard_map/ppermute | solution.py:178
  168.0 18.7 %collective-permute-start.14 = (bf16[4,192,192]{2,1,0:T(8,128)(2,1)}, bf16[4,192,192]{2,1,0:T(8,128)(2,1)}, u32[]{:S(2)}, u32[]{:S(2)}) collective-permute-start(bf16[4,192,192]{2,1,0:T(8,128)(2,1)} %get-tuple-element.57), channel_id=1, source_target_pairs={{0,16},{8,24},{16,0},{24,8},{1,17},{9,25},{17,1},{25,9},{2,18},{10... | collective-permute-start | bytes 884744 | tf_op jit(solution)/shard_map/ppermute | solution.py:178
  169.7 17.0 %collective-permute-start.15 = (bf16[4,192,192]{2,1,0:T(8,128)(2,1)}, bf16[4,192,192]{2,1,0:T(8,128)(2,1)}, u32[]{:S(2)}, u32[]{:S(2)}) collective-permute-start(bf16[4,192,192]{2,1,0:T(8,128)(2,1)} %get-tuple-element.58), channel_id=1, source_target_pairs={{0,8},{8,0},{16,24},{24,16},{1,9},{9,1},{17,25},{25,17},{2,10},{10... | collective-permute-start | bytes 884744 | tf_op jit(solution)/shard_map/ppermute | solution.py:178
  169.8 52.4 %collective-permute-start.20 = (bf16[2,192,768]{2,1,0:T(8,128)(2,1)S(1)}, bf16[2,192,768]{2,1,0:T(8,128)(2,1)}, u32[]{:S(2)}, u32[]{:S(2)}) collective-permute-start(bf16[2,192,768]{2,1,0:T(8,128)(2,1)S(1)} %copy-done.5), channel_id=1, source_target_pairs={{0,16},{8,24},{16,0},{24,8},{1,17},{9,25},{17,1},{25,9},{2,18},{10... | collective-permute-start | bytes 1769480 | tf_op jit(solution)/shard_map/ppermute | solution.py:178
  180.6 43.3 %collective-permute-start.29 = (bf16[2,192,768]{2,1,0:T(8,128)(2,1)}, bf16[2,192,768]{2,1,0:T(8,128)(2,1)}, u32[]{:S(2)}, u32[]{:S(2)}) collective-permute-start(bf16[2,192,768]{2,1,0:T(8,128)(2,1)} %get-tuple-element.66.refs_8_), channel_id=1, source_target_pairs={{0,16},{8,24},{16,0},{24,8},{1,17},{9,25},{17,1},{25,9},{2,18},{10... | collective-permute-start | bytes 1769480 | tf_op jit(solution)/shard_map/ppermute | solution.py:178
  185.6 28.3 %collective-permute-start.26 = (bf16[4,192,192]{2,1,0:T(8,128)(2,1)}, bf16[4,192,192]{2,1,0:T(8,128)(2,1)S(1)}, u32[]{:S(2)}, u32[]{:S(2)}) collective-permute-start(bf16[4,192,192]{2,1,0:T(8,128)(2,1)} %get-tuple-element.63), channel_id=1, source_target_pairs={{0,16},{8,24},{16,0},{24,8},{1,17},{9,25},{17,1},{25,9},{2,18},{10... | collective-permute-start | bytes 884744 | tf_op jit(solution)/shard_map/ppermute | solution.py:178
  186.7 27.2 %collective-permute-start.27 = (bf16[4,192,192]{2,1,0:T(8,128)(2,1)}, bf16[4,192,192]{2,1,0:T(8,128)(2,1)S(1)}, u32[]{:S(2)}, u32[]{:S(2)}) collective-permute-start(bf16[4,192,192]{2,1,0:T(8,128)(2,1)} %get-tuple-element.64), channel_id=1, source_target_pairs={{0,8},{8,0},{16,24},{24,16},{1,9},{9,1},{17,25},{25,17},{2,10},{10... | collective-permute-start | bytes 884744 | tf_op jit(solution)/shard_map/ppermute | solution.py:178
  186.7 35.0 %collective-permute-start.28 = (bf16[4,192,192]{2,1,0:T(8,128)(2,1)}, bf16[4,192,192]{2,1,0:T(8,128)(2,1)S(1)}, u32[]{:S(2)}, u32[]{:S(2)}) collective-permute-start(bf16[4,192,192]{2,1,0:T(8,128)(2,1)} %get-tuple-element.65), channel_id=1, source_target_pairs={{0,24},{8,16},{16,8},{24,0},{1,25},{9,17},{17,9},{25,1},{2,26},{10... | collective-permute-start | bytes 884744 | tf_op jit(solution)/shard_map/ppermute | solution.py:178
  189.3 63.9 %slice-start = ((s8[6291456]{0:T(1024)(128)(4,1)}), s8[4194304]{0:T(1024)(128)(4,1)S(1)}, s32[]{:S(2)}) async-start(s8[6291456]{0:T(1024)(128)(4,1)} %bitcast.121), calls=%async_computation.4 | async-start | bytes 8388608
  191.2 31.0 %copy-start.4 = (bf16[2,192,768]{2,1,0:T(8,128)(2,1)S(1)}, bf16[2,192,768]{2,1,0:T(8,128)(2,1)}, u32[]{:S(2)}) copy-start(bf16[2,192,768]{2,1,0:T(8,128)(2,1)} %get-tuple-element.61.refs_9_) | copy-start | bytes 1769476
  191.2 62.0 %slice-start.1 = ((s8[6291456]{0:T(1024)(128)(4,1)}), s8[2097152]{0:T(1024)(128)(4,1)S(1)}, s32[]{:S(2)}) async-start(s8[6291456]{0:T(1024)(128)(4,1)} %bitcast.121), calls=%async_computation.5 | async-start | bytes 4194304
  213.9 35.6 %copy-start.20 = (bf16[4,192,192]{2,1,0:T(8,128)(2,1)}, bf16[4,192,192]{2,1,0:T(8,128)(2,1)S(1)}, u32[]{:S(2)}) copy-start(bf16[4,192,192]{2,1,0:T(8,128)(2,1)S(1)} %collective-permute-done.26.refs_1_) | copy-start | bytes 884740
  213.9 33.6 %collective-permute-start.31 = (bf16[2,192,768]{2,1,0:T(8,128)(2,1)}, bf16[2,192,768]{2,1,0:T(8,128)(2,1)S(1)}, u32[]{:S(2)}, u32[]{:S(2)}) collective-permute-start(bf16[2,192,768]{2,1,0:T(8,128)(2,1)} %get-tuple-element.66.refs_8_), channel_id=1, source_target_pairs={{0,8},{8,0},{16,24},{24,16},{1,9},{9,1},{17,25},{25,17},{2,10},{10... | collective-permute-start | bytes 1769480 | tf_op jit(solution)/shard_map/ppermute | solution.py:178
  213.9 35.6 %copy-start.21 = (bf16[4,192,192]{2,1,0:T(8,128)(2,1)}, bf16[4,192,192]{2,1,0:T(8,128)(2,1)S(1)}, u32[]{:S(2)}) copy-start(bf16[4,192,192]{2,1,0:T(8,128)(2,1)S(1)} %collective-permute-done.27.refs_2_) | copy-start | bytes 884740
  213.9 33.0 %collective-permute-start.30 = (bf16[2,192,768]{2,1,0:T(8,128)(2,1)S(1)}, bf16[2,192,768]{2,1,0:T(8,128)(2,1)S(1)}, u32[]{:S(2)}, u32[]{:S(2)}) collective-permute-start(bf16[2,192,768]{2,1,0:T(8,128)(2,1)S(1)} %copy-done.6), channel_id=1, source_target_pairs={{0,16},{8,24},{16,0},{24,8},{1,17},{9,25},{17,1},{25,9},{2,18},{10... | collective-permute-start | bytes 1769480 | tf_op jit(solution)/shard_map/ppermute | solution.py:178
  221.7 25.8 %collective-permute-start.32 = (bf16[2,192,768]{2,1,0:T(8,128)(2,1)S(1)}, bf16[2,192,768]{2,1,0:T(8,128)(2,1)S(1)}, u32[]{:S(2)}, u32[]{:S(2)}) collective-permute-start(bf16[2,192,768]{2,1,0:T(8,128)(2,1)S(1)} %copy-done.6), channel_id=1, source_target_pairs={{0,8},{8,0},{16,24},{24,16},{1,9},{9,1},{17,25},{25,17},{2,10},{10... | collective-permute-start | bytes 1769480 | tf_op jit(solution)/shard_map/ppermute | solution.py:178
  222.1 24.8 %collective-permute-start.21 = (bf16[2,192,768]{2,1,0:T(8,128)(2,1)S(1)}, bf16[2,192,768]{2,1,0:T(8,128)(2,1)}, u32[]{:S(2)}, u32[]{:S(2)}) collective-permute-start(bf16[2,192,768]{2,1,0:T(8,128)(2,1)S(1)} %copy-done.4), channel_id=1, source_target_pairs={{0,16},{8,24},{16,0},{24,8},{1,17},{9,25},{17,1},{25,9},{2,18},{10... | collective-permute-start | bytes 1769480 | tf_op jit(solution)/shard_map/ppermute | solution.py:178
  223.9 24.1 %collective-permute-start.33 = (bf16[2,192,768]{2,1,0:T(8,128)(2,1)}, bf16[2,192,768]{2,1,0:T(8,128)(2,1)S(1)}, u32[]{:S(2)}, u32[]{:S(2)}) collective-permute-start(bf16[2,192,768]{2,1,0:T(8,128)(2,1)} %collective-permute-done.29.refs_10_), channel_id=1, source_target_pairs={{0,8},{8,0},{16,24},{24,16},{1,9},{9,1},{17,25},{25,17},{2,10},{10... | collective-permute-start | bytes 1769480 | tf_op jit(solution)/shard_map/ppermute | solution.py:178
  225.2 28.0 %copy-start.27 = (bf16[48,512]{1,0:T(8,128)(2,1)S(1)}, bf16[48,512]{1,0:T(8,128)(2,1)}, u32[]{:S(2)}) copy-start(bf16[48,512]{1,0:T(8,128)(2,1)} %copy-done.26) | copy-start | bytes 147460
  225.2 28.0 %copy-start.32 = (bf16[48,512]{1,0:T(8,128)(2,1)S(1)}, bf16[48,512]{1,0:T(8,128)(2,1)}, u32[]{:S(2)}) copy-start(bf16[48,512]{1,0:T(8,128)(2,1)} %copy-done.31) | copy-start | bytes 147460
  246.9 17.6 %collective-permute-start.22 = (bf16[2,192,768]{2,1,0:T(8,128)(2,1)S(1)}, bf16[2,192,768]{2,1,0:T(8,128)(2,1)S(1)}, u32[]{:S(2)}, u32[]{:S(2)}) collective-permute-start(bf16[2,192,768]{2,1,0:T(8,128)(2,1)S(1)} %copy-done.5), channel_id=1, source_target_pairs={{0,8},{8,0},{16,24},{24,16},{1,9},{9,1},{17,25},{25,17},{2,10},{10... | collective-permute-start | bytes 1769480 | tf_op jit(solution)/shard_map/ppermute | solution.py:178
  246.9 17.6 %collective-permute-start.23 = (bf16[2,192,768]{2,1,0:T(8,128)(2,1)S(1)}, bf16[2,192,768]{2,1,0:T(8,128)(2,1)S(1)}, u32[]{:S(2)}, u32[]{:S(2)}) collective-permute-start(bf16[2,192,768]{2,1,0:T(8,128)(2,1)S(1)} %copy-done.4), channel_id=1, source_target_pairs={{0,8},{8,0},{16,24},{24,16},{1,9},{9,1},{17,25},{25,17},{2,10},{10... | collective-permute-start | bytes 1769480 | tf_op jit(solution)/shard_map/ppermute | solution.py:178
  247.5 17.8 %collective-permute-start.24 = (bf16[2,192,768]{2,1,0:T(8,128)(2,1)}, bf16[2,192,768]{2,1,0:T(8,128)(2,1)}, u32[]{:S(2)}, u32[]{:S(2)}) collective-permute-start(bf16[2,192,768]{2,1,0:T(8,128)(2,1)} %collective-permute-done.20.refs_10_), channel_id=1, source_target_pairs={{0,8},{8,0},{16,24},{24,16},{1,9},{9,1},{17,25},{25,17},{2,10},{10... | collective-permute-start | bytes 1769480 | tf_op jit(solution)/shard_map/ppermute | solution.py:178
  247.6 17.7 %collective-permute-start.25 = (bf16[2,192,768]{2,1,0:T(8,128)(2,1)}, bf16[2,192,768]{2,1,0:T(8,128)(2,1)}, u32[]{:S(2)}, u32[]{:S(2)}) collective-permute-start(bf16[2,192,768]{2,1,0:T(8,128)(2,1)} %collective-permute-done.21.refs_11_), channel_id=1, source_target_pairs={{0,8},{8,0},{16,24},{24,16},{1,9},{9,1},{17,25},{25,17},{2,10},{10... | collective-permute-start | bytes 1769480 | tf_op jit(solution)/shard_map/ppermute | solution.py:178
  248.0 4.3 %collective-permute-start.34 = (bf16[2,192,768]{2,1,0:T(8,128)(2,1)S(1)}, bf16[2,192,768]{2,1,0:T(8,128)(2,1)S(1)}, u32[]{:S(2)}, u32[]{:S(2)}) collective-permute-start(bf16[2,192,768]{2,1,0:T(8,128)(2,1)S(1)} %collective-permute-done.30.refs_11_), channel_id=1, source_target_pairs={{0,8},{8,0},{16,24},{24,16},{1,9},{9,1},{17,25},{25,17},{2,10},{10... | collective-permute-start | bytes 1769480 | tf_op jit(solution)/shard_map/ppermute | solution.py:178
  253.2 11.3 %collective-permute-start.16 = (bf16[4,192,192]{2,1,0:T(8,128)(2,1)}, bf16[4,192,192]{2,1,0:T(8,128)(2,1)S(1)}, u32[]{:S(2)}, u32[]{:S(2)}) collective-permute-start(bf16[4,192,192]{2,1,0:T(8,128)(2,1)} %get-tuple-element.59), channel_id=1, source_target_pairs={{0,24},{8,16},{16,8},{24,0},{1,25},{9,17},{17,9},{25,1},{2,26},{10... | collective-permute-start | bytes 884744 | tf_op jit(solution)/shard_map/ppermute | solution.py:178
  (29 other events, 156.5 us)
Sparse Core Ops, SparseCore 0:
  38.0 36.8 all-gather.4
  76.5 29.0 all-gather.2
